TPU v7x, 32 devices: a whole 2x2x4 slice. The times are simulated.
32 devices in a mesh: groups: 2 (over y), shots: 4 (over z), dom: 2 (over x), sub: 2 (over core).
Axes of the slice: x: 2, y: 2, z: 4, core: 2. Of those that a mesh axis runs over, the one named last changes fastest.
Arguments:
- velocity: float32 [64, 16, 256], P(('groups', 'shots'), 'dom', 'sub'), parts along dimension 0, may hold values from 0.15 to 0.4
- wave_prev: bfloat16 [8, 32, 16, 256], P(('groups', 'shots'), None, 'dom', 'sub'), parts along dimension 0, may hold values from -6 to 6
- wave_now: bfloat16 [8, 32, 16, 256], P(('groups', 'shots'), None, 'dom', 'sub'), parts along dimension 0, may hold values from -6 to 6
- adj_next: bfloat16 [8, 32, 16, 256], P(('groups', 'shots'), None, 'dom', 'sub'), parts along dimension 0, may hold values from -6 to 6
- adj_now: bfloat16 [8, 32, 16, 256], P(('groups', 'shots'), None, 'dom', 'sub'), parts along dimension 0, may hold values from -6 to 6
- sponge: int32 [32, 16, 256], P(None, 'dom', 'sub'), may hold values 0 or 1
- wavelet: float32 [8, 6], P(('groups', 'shots')), parts along dimension 0, may hold values from -12 to 12
- src_pos: int32 [8], P(('groups', 'shots')), parts along dimension 0, may hold values from 0 to 4095
- rec_pos: int32 [8, 256], P(('groups', 'shots')), parts along dimension 0, may hold values from 0 to 4095
- observed: float32 [8, 4, 256], P(('groups', 'shots')), parts along dimension 0, may hold values from -6 to 6
Outputs:
- direction: float32 [64, 16, 256], P(('groups', 'shots'), 'dom', 'sub'), parts along dimension 0
- wave_out: float32 [8, 32, 16, 256], P(('groups', 'shots'), None, 'dom', 'sub'), parts along dimension 0
There are 2 independent parts, one for each index of `groups`. A program takes and returns all parts, laid end to end along the dimension named above; an argument that names none is the same for every part. Nothing has to cross between parts.
Inputs may be any that keep to these rules, and one draw needn't show every extreme that they name: `src_pos`: a horizontal position x * 256 + y on the grid. `rec_pos`: horizontal positions x * 256 + y on the grid, possibly repeated.
All inputs are finite; a program needn't handle non-finite values. Where the computation divides by a largest or mean magnitude, that divisor is 1e-20 or more. No bound on the sum of `sponge` on one device may be relied on, other than what follows from the above.
Results may differ from a plain program's by a relative error of at most 0.0003.
Values sent between devices are 32-bit elements; how exact they have to be, the bound alone decides.
A program may use at most 64 MiB of HBM per device.

v0:
```python
import functools

import jax
import jax.numpy as jnp
import numpy as np
from jax import lax
from jax.experimental import pallas as pl
from jax.experimental.pallas import tpu as pltpu
from jax.sharding import PartitionSpec as P

NF = 4
NFIN = 2

coeffs = (-205.0 / 72.0, 8.0 / 5.0, -1.0 / 5.0, 8.0 / 315.0, -1.0 / 560.0)
damp_rate = 0.2
step_rate = 0.1
floor_share = 0.5
src_depth = 2
rec_depth = 1
reach = 4

MESH = pl.DeviceIdType.MESH
F32 = jnp.float32
BF16 = jnp.bfloat16


def band(size, period):
    full = np.zeros((size, size), np.float64)
    for row in range(size):
        for k in range(1, reach + 1):
            for col in (row - k, row + k):
                if 0 <= col < size and col // period == row // period:
                    full[row, col] = coeffs[k]
    high = full.astype(np.float32).astype(BF16)
    low = (full - high.astype(np.float64)).astype(np.float32).astype(BF16)
    return high, low


def split(value):
    high = value.astype(BF16)
    low = (value - high.astype(F32)).astype(BF16)
    return high, low


def copies_needed(shots, dom, sub):
    fields = 5 * ((dom - 1) + dom * (sub - 1))
    slabs = 2 * (shots * dom * sub)
    return fields + slabs + 2 * shots


def kernel(
    sizes,
    vel_ref, prev_ref, now_ref, adjn_ref, adj_ref, sponge_ref, amp_ref, src_ref, rec_ref, obs_ref,
    bh_ref, bl_ref, kh_ref, kl_ref,
    both_ref,
    U, L, V, SP, IV, QV, KP, ACC, PC, OB, CNT, GI, GR, ss, rs,
):
    shots, dom, sub, depth, rows, cols, owned, zb = sizes
    X, Y = dom * rows, sub * cols
    s = lax.axis_index("shots")
    d = lax.axis_index("dom")
    c = lax.axis_index("sub")
    counts = {"shots": shots, "dom": dom, "sub": sub}
    me = {"shots": s, "dom": d, "sub": c}
    tickets = [0]
    sent = []

    def peer(axis, j):
        return lax.rem(me[axis] + j, counts[axis])

    def source(axis, j):
        return lax.rem(me[axis] + (counts[axis] - j), counts[axis])

    def xs(i):
        return pl.ds(pl.multiple_of(i * rows, rows), rows)

    def ys(i):
        return pl.ds(pl.multiple_of(i * cols, cols), cols)

    def send(src, dst, axis, j):
        idx = tickets[0]
        tickets[0] += 1
        copy = pltpu.make_async_remote_copy(
            src_ref=src, dst_ref=dst, send_sem=ss.at[idx], recv_sem=rs.at[idx],
            device_id={axis: peer(axis, j)}, device_id_type=MESH,
        )
        copy.start()
        sent.append(copy)
        return idx

    def arrived(idx, dst, axis):
        pltpu.make_async_remote_copy(
            src_ref=dst, dst_ref=dst, send_sem=ss.at[idx], recv_sem=rs.at[idx],
            device_id={axis: peer(axis, 1)}, device_id_type=MESH,
        ).wait_recv()

    def field_send(place):
        hops = [(i, send(place(d, c), place(d, c), "dom", i)) for i in range(1, dom)]
        cross = [(0, k, send(place(d, c), place(d, c), "sub", k)) for k in range(1, sub)]
        return hops, cross

    def field_relay(place, state):
        hops, cross = state
        for i, idx in hops:
            here = place(source("dom", i), c)
            arrived(idx, here, "dom")
            cross += [(i, k, send(here, here, "sub", k)) for k in range(1, sub)]

    def field_done(place, state):
        for i, k, idx in state[1]:
            arrived(idx, place(source("dom", i), source("sub", k)), "sub")

    def slab_send(place, first, second):
        own = place({"shots": s, "dom": d}, c)
        state = {
            "one": [(i, send(own, own, first, i)) for i in range(1, counts[first])],
            "two": [(0, j, send(own, own, second, j)) for j in range(1, counts[second])],
            "cross": [(0, 0, k, send(own, own, "sub", k)) for k in range(1, sub)],
        }
        return state

    def slab_relay(place, state, first, second):
        for i, idx in state["one"]:
            here = place({first: source(first, i), second: me[second]}, c)
            arrived(idx, here, first)
            state["two"] += [(i, j, send(here, here, second, j)) for j in range(1, counts[second])]
            state["cross"] += [(i, 0, k, send(here, here, "sub", k)) for k in range(1, sub)]

    def slab_relay_two(place, state, first, second):
        for i, j, idx in state["two"]:
            here = place({first: source(first, i), second: source(second, j)}, c)
            arrived(idx, here, second)
            state["cross"] += [(i, j, k, send(here, here, "sub", k)) for k in range(1, sub)]

    def slab_done(place, state, first, second):
        for i, j, k, idx in state["cross"]:
            arrived(idx, place({first: source(first, i), second: source(second, j)}, source("sub", k)), "sub")

    def in_field(ref, n):
        return lambda i, k: ref.at[n, pl.ds(reach, depth), xs(i), ys(k)]

    def in_whole(ref):
        return lambda i, k: ref.at[:, xs(i), ys(k)]

    def in_slab(ref):
        return lambda at, k: ref.at[pl.ds(at["shots"] * owned, owned), xs(at["dom"]), ys(k)]

    def lateral(ref, n):
        for b in range(depth // zb):
            lo = reach + b * zb
            u = ref[n, lo : lo + zb].reshape(zb * X, Y)
            uh, ul = split(u)
            acc = jnp.dot(uh, bh_ref[...], preferred_element_type=F32)
            acc = acc + jnp.dot(kh_ref[...], uh, preferred_element_type=F32)
            acc = acc + jnp.dot(uh, bl_ref[...], preferred_element_type=F32)
            acc = acc + jnp.dot(ul, bh_ref[...], preferred_element_type=F32)
            acc = acc + jnp.dot(kl_ref[...], uh, preferred_element_type=F32)
            acc = acc + jnp.dot(kh_ref[...], ul, preferred_element_type=F32)
            ACC[b * zb : (b + 1) * zb] = acc.reshape(zb, X, Y)

    barrier = pltpu.get_barrier_semaphore()
    for axis, count in counts.items():
        for j in range(1, count):
            pl.semaphore_signal(barrier, inc=1, device_id={axis: peer(axis, j)}, device_id_type=MESH)

    own_x, own_y = xs(d), ys(c)
    V[pl.ds(s * owned, owned), own_x, own_y] = vel_ref[...]
    U[1, pl.ds(reach, depth), own_x, own_y] = now_ref[0].astype(F32)
    U[0, pl.ds(reach, depth), own_x, own_y] = prev_ref[0].astype(F32)
    SP[:, own_x, own_y] = sponge_ref[...].astype(F32)
    L[1, pl.ds(reach, depth), own_x, own_y] = adj_ref[0].astype(F32)
    L[0, pl.ds(reach, depth), own_x, own_y] = adjn_ref[0].astype(F32)

    pl.semaphore_wait(barrier, sum(counts.values()) - 3)

    vel_state = slab_send(in_slab(V), "dom", "shots")
    now_state = field_send(in_field(U, 1))
    sp_state = field_send(in_whole(SP))
    prev_state = field_send(in_field(U, 0))
    adj_state = field_send(in_field(L, 1))
    adjn_state = field_send(in_field(L, 0))

    edge = jnp.zeros((reach, X, Y), F32)
    for ref in (U, L):
        for n in range(ref.shape[0]):
            ref[n, 0:reach] = edge
            ref[n, reach + depth : 2 * reach + depth] = edge
    pos = rec_ref[...]
    row_of = jnp.zeros_like(pos)
    for x in range(1, X):
        row_of = row_of + (pos >= x * Y).astype(jnp.int32)
    col_of = pos - row_of * Y
    nrec = pos.shape[1]
    x_hot = (lax.broadcasted_iota(jnp.int32, (X, nrec), 0) == row_of).astype(F32)
    y_hot = (lax.broadcasted_iota(jnp.int32, (Y, nrec), 0) == col_of).astype(F32).astype(BF16)

    def spread(lhs):
        return lax.dot_general(lhs, y_hot, (((1,), (1,)), ((), ())), preferred_element_type=F32)

    CNT[...] = spread(x_hot.astype(BF16))
    slab_relay(in_slab(V), vel_state, "dom", "shots")
    for n in range(NF):
        vals = x_hot * obs_ref[0, n : n + 1, :]
        a = vals.astype(BF16)
        b, rest = split(vals - a.astype(F32))
        OB[n] = spread(a) + spread(b) + spread(rest)
    flat = lax.broadcasted_iota(jnp.int32, (X, Y), 0) * Y + lax.broadcasted_iota(jnp.int32, (X, Y), 1)
    src_hot = (flat == src_ref[0]).astype(F32)

    field_relay(in_field(U, 1), now_state)
    field_relay(in_whole(SP), sp_state)
    field_done(in_field(U, 1), now_state)
    lateral(U, 1)
    slab_relay_two(in_slab(V), vel_state, "dom", "shots")
    field_relay(in_field(U, 0), prev_state)
    slab_done(in_slab(V), vel_state, "dom", "shots")
    field_done(in_whole(SP), sp_state)
    for z in range(depth):
        damp = damp_rate * SP[z]
        inv = 1.0 / (1.0 + damp)
        IV[z] = inv
        QV[z] = (1.0 - damp) * inv
        vel = V[z]
        KP[z] = vel * vel * inv
    field_done(in_field(U, 0), prev_state)

    def level(ref, n, z, xr, yr, plane):
        mid = ref[n, reach + z, xr, yr]
        lap = ACC[z, xr, yr] + (3.0 * coeffs[0]) * mid
        for k in range(1, reach + 1):
            lap = lap + coeffs[k] * (ref[n, reach + z + k, xr, yr] + ref[n, reach + z - k, xr, yr])
        inv = IV[z, xr, yr]
        drive = 2.0 * mid if plane is None else 2.0 * mid + plane
        return inv * drive - QV[z, xr, yr] * ref[n - 1, reach + z, xr, yr] + KP[z, xr, yr] * lap

    whole_x, whole_y = slice(None), slice(None)

    def advance(ref, n, plane, at, ready=False):
        if not ready:
            lateral(ref, n)
        for z in range(depth):
            ref[n + 1, reach + z] = level(ref, n, z, whole_x, whole_y, plane if z == at else None)

    for n in range(NF):
        advance(U, n + 1, src_hot * amp_ref[0, n], src_depth, n == 0)
        if n == max(0, NF - 3):
            field_relay(in_field(L, 1), adj_state)
        if n == max(0, NF - 2):
            field_relay(in_field(L, 0), adjn_state)

    for z in range(depth):
        illum = None
        for n in range(NF):
            value = U[n + 2, reach + z, own_x, own_y]
            illum = value * value if illum is None else illum + value * value
        GI[1, z] = illum
    field_done(in_field(L, 1), adj_state)
    lateral(L, 1)
    far_first = sorted(range(1, shots), key=lambda j: -min(j, shots - j))

    def to_owners(f):
        return [
            (j, send(GI.at[f, pl.ds(peer("shots", j) * owned, owned)], GR.at[j - 1, f], "shots", j))
            for j in far_first
        ]

    illum_parts = to_owners(1)
    field_done(in_field(L, 0), adjn_state)

    for n in range(NF, 0, -1):
        plane = CNT[...] * U[n + 1, reach + rec_depth] - OB[n - 1]
        advance(L, NF + 1 - n, plane, rec_depth, n == NF)

    for z in range(depth):
        at = (reach + z, own_x, own_y)
        u = [U[(n,) + at] for n in range(NF + 2)]
        grad = None
        for n in range(NF):
            term = L[(NF + 1 - n,) + at] * (u[n + 2] - 2.0 * u[n + 1] + u[n])
            grad = term if grad is None else grad + term
        GI[0, z] = grad

    grad_parts = to_owners(0)
    lateral(U, NF + 1)
    below = GI[1, pl.ds(s * owned, owned)] + floor_share * shots
    for j, idx in illum_parts:
        arrived(idx, GR.at[j - 1, 1], "shots")
        below = below + GR[j - 1, 1]
    above = GI[0, pl.ds(s * owned, owned)]
    for j, idx in grad_parts:
        arrived(idx, GR.at[j - 1, 0], "shots")
        above = above + GR[j - 1, 0]
    mine = above / below
    PC[pl.ds(s * owned, owned), own_x, own_y] = mine
    pc_state = slab_send(in_slab(PC), "shots", "dom")
    slab_relay(in_slab(PC), pc_state, "shots", "dom")
    slab_relay_two(in_slab(PC), pc_state, "shots", "dom")
    slab_done(in_slab(PC), pc_state, "shots", "dom")
    top = jnp.abs(PC[0])
    for z in range(1, depth):
        top = jnp.maximum(top, jnp.abs(PC[z]))
    peak = jnp.max(jnp.max(top, axis=0, keepdims=True), axis=1, keepdims=True)
    scale = 1.0 / (peak + 1e-06)
    both_ref[0:owned] = mine * scale
    for z in range(depth):
        updated = V[z] * (1.0 - step_rate * (PC[z] * scale))
        KP[z] = updated * updated * IV[z]
    for n in range(NFIN):
        plane = src_hot * amp_ref[0, NF + n]
        if n > 0:
            lateral(U, NF + 1 + n)
        if n < NFIN - 1:
            for z in range(depth):
                U[NF + 2 + n, reach + z] = level(
                    U, NF + 1 + n, z, whole_x, whole_y, plane if z == src_depth else None
                )
        else:
            for z in range(depth):
                both_ref[owned + z] = level(U, NF + 1 + n, z, own_x, own_y, None)
            ACC[0] = plane * IV[src_depth]
            both_ref[owned + src_depth] += ACC[0, own_x, own_y]
    for copy in sent:
        copy.wait_send()


def part(both_ref, dir_ref, out_ref):
    owned = dir_ref.shape[0]
    dir_ref[...] = both_ref[0:owned]
    out_ref[0] = both_ref[owned:]


def solution(mesh):
    shots, dom, sub = mesh.shape["shots"], mesh.shape["dom"], mesh.shape["sub"]

    def shards(velocity, wave_prev, wave_now, adj_next, adj_now, sponge, wavelet, src_pos, rec_pos, observed):
        depth, rows, cols = sponge.shape
        owned = velocity.shape[0]
        X, Y = dom * rows, sub * cols
        zb = min(depth, max(1, 256 // X))
        bh, bl = band(Y, Y)
        kh, kl = band(zb * X, X)
        vm = pl.BlockSpec(memory_space=pltpu.VMEM)
        sm = pl.BlockSpec(memory_space=pltpu.SMEM)
        whole = pltpu.VMEM((depth, X, Y), F32)
        n_sems = copies_needed(shots, dom, sub)
        both = pl.pallas_call(
            functools.partial(kernel, (shots, dom, sub, depth, rows, cols, owned, zb)),
            out_shape=jax.ShapeDtypeStruct((owned + depth, rows, cols), F32),
            in_specs=[vm] * 6 + [sm, sm] + [vm] * 6,
            out_specs=vm,
            scratch_shapes=[
                pltpu.VMEM((NF + NFIN + 1, depth + 2 * reach, X, Y), F32),
                pltpu.VMEM((NF + 2, depth + 2 * reach, X, Y), F32),
                whole, whole, whole, whole, whole, whole, whole,
                pltpu.VMEM((NF, X, Y), F32),
                pltpu.VMEM((X, Y), F32),
                pltpu.VMEM((2, depth, rows, cols), F32),
                pltpu.VMEM((max(1, shots - 1), 2, owned, rows, cols), F32),
                pltpu.SemaphoreType.DMA((n_sems,)),
                pltpu.SemaphoreType.DMA((n_sems,)),
            ],
            compiler_params=pltpu.CompilerParams(
                collective_id=0, has_side_effects=True, vmem_limit_bytes=56 * 1024 * 1024
            ),
        )(velocity, wave_prev, wave_now, adj_next, adj_now, sponge, wavelet, src_pos, rec_pos, observed,
          jnp.asarray(bh), jnp.asarray(bl), jnp.asarray(kh), jnp.asarray(kl))
        return tuple(pl.pallas_call(
            part,
            out_shape=(
                jax.ShapeDtypeStruct((owned, rows, cols), F32),
                jax.ShapeDtypeStruct((1, depth, rows, cols), F32),
            ),
            in_specs=[vm],
            out_specs=(vm, vm),
        )(both))

    return jax.shard_map(
        shards,
        mesh=mesh,
        in_specs=(
            P(("groups", "shots"), "dom", "sub"),
            P(("groups", "shots"), None, "dom", "sub"),
            P(("groups", "shots"), None, "dom", "sub"),
            P(("groups", "shots"), None, "dom", "sub"),
            P(("groups", "shots"), None, "dom", "sub"),
            P(None, "dom", "sub"),
            P(("groups", "shots"), None),
            P(("groups", "shots")),
            P(("groups", "shots"), None),
            P(("groups", "shots"), None, None),
        ),
        out_specs=(
            P(("groups", "shots"), "dom", "sub"),
            P(("groups", "shots"), None, "dom", "sub"),
        ),
        check_vma=False,
    )
```

profile of v0, /device:TPU:1, one launch (start us, length us, event | category | flops | bytes accessed | tf_op | source)
XLA Modules:
  0.0 46.1 jit_solution(10034310762399797786)
XLA Ops:
  1.3 43.2 %shard_map.149.both_ref = f32[40,8,128]{2,1,0:T(8,128)} custom-call(f32[8,8,128]{2,1,0:T(8,128)} %vel_ref.1, bf16[1,32,8,128]{3,2,1,0:T(8,128)(2,1)} %prev_ref.1, bf16[1,32,8,128]{3,2,1,0:T(8,128)(2,1)} %now_ref.1, bf16[1,32,8,128]{3,2,1,0:T(8,128)(2,1)} %adjn_ref.1, bf16[1,32,8,128]{3,2,1,0:T(8,128)(2,1)} %adj_ref.1, s32[32,8,128]{2,1,0:T(8,128)} %sponge_ref.1, ...), custom_call_target="tpu_custom_call" | custom-call | tf_op jit(solution)/shard_map/pallas_call | solution.py:346
  44.5 1.6 %shard_map.150 = (f32[8,8,128]{2,1,0:T(8,128)}, f32[1,32,8,128]{3,2,1,0:T(8,128)}) custom-call(f32[40,8,128]{2,1,0:T(8,128)} %shard_map.149.both_ref), custom_call_target="tpu_custom_call" | custom-call | tf_op jit(solution)/shard_map/pallas_call | solution.py:367
where the time goes:
time: 46.3 us; the launch traced here: 46.1 us
  Pallas kernels  44.8 us (97%)
  between operations  1.29 us (3%)
    pallas_call x1, Pallas kernels, shards(): pl.pallas_call(functools.partial(kernel, (shots, dom, sub, depth, rows, c...  43.2 us
    pallas_call x1, Pallas kernels, shards(): pl.pallas_call(part, out_shape=(jax.ShapeDtypeStruct((owned, rows, cols),...  1.59 us

commit v1 on v0

v1 whole, which is shorter than its diff:
```python
import functools

import jax
import jax.numpy as jnp
import numpy as np
from jax import lax
from jax.experimental import pallas as pl
from jax.experimental.pallas import tpu as pltpu
from jax.sharding import PartitionSpec as P

VM_MAIN = 48 * 1024 * 1024
VM_PART = 2 * 1024 * 1024
NF = 4
NFIN = 2

coeffs = (-205.0 / 72.0, 8.0 / 5.0, -1.0 / 5.0, 8.0 / 315.0, -1.0 / 560.0)
damp_rate = 0.2
step_rate = 0.1
floor_share = 0.5
src_depth = 2
rec_depth = 1
reach = 4
unit = coeffs[1]
centre = 3.0 * coeffs[0] / unit

MESH = pl.DeviceIdType.MESH
F32 = jnp.float32
BF16 = jnp.bfloat16


def along_y(size):
    full = np.zeros((size, size), np.float32)
    for row in range(size):
        for k in range(1, reach + 1):
            for col in (row - k, row + k):
                if 0 <= col < size:
                    full[row, col] = coeffs[k] / unit
    return full.astype(BF16)


def along_zx(zb, X):
    full = np.zeros((zb, X, zb + 2 * reach, X), np.float32)
    for z in range(zb):
        for x in range(X):
            for k in range(1, reach + 1):
                for other in (-k, k):
                    full[z, x, z + reach + other, x] = coeffs[k] / unit
                    if 0 <= x + other < X:
                        full[z, x, z + reach, x + other] = coeffs[k] / unit
    return full.reshape(zb * X, (zb + 2 * reach) * X).astype(BF16)


def split(value):
    high = value.astype(BF16)
    low = (value - high.astype(F32)).astype(BF16)
    return high, low


def copies_needed(shots, dom, sub):
    fields = 5 * ((dom - 1) + dom * (sub - 1))
    slab = shots * dom * sub
    back = (shots * dom - 1) + shots * (sub - 1) + (sub - 1)
    return fields + slab + 2 * (shots - 1) + back


def kernel(
    sizes,
    vel_in, prev_in, now_in, adjn_in, adj_in, sponge_in, amp_in, src_ref, rec_in, obs_in, ym_in, zx_in,
    both_ref,
    vel_ref, prev_ref, now_ref, adjn_ref, adj_ref, sponge_ref, amp_ref, rec_ref, obs_ref, ym_ref, zx_ref,
    U, L, H, V, SP, IV, KP, ACC, PC, PK, OB, CNT, SR, GI, GR, ss, rs, ls,
):
    shots, dom, sub, depth, rows, cols, owned, zb = sizes
    X, Y = dom * rows, sub * cols
    s = lax.axis_index("shots")
    d = lax.axis_index("dom")
    c = lax.axis_index("sub")
    counts = {"shots": shots, "dom": dom, "sub": sub}
    me = {"shots": s, "dom": d, "sub": c}
    tickets = [0]
    sent = []

    def peer(axis, j):
        return lax.rem(me[axis] + j, counts[axis])

    def source(axis, j):
        return lax.rem(me[axis] + (counts[axis] - j), counts[axis])

    def xs(i):
        return pl.ds(pl.multiple_of(i * rows, rows), rows)

    def ys(i):
        return pl.ds(pl.multiple_of(i * cols, cols), cols)

    def send_to(src, dst, shifts):
        idx = tickets[0]
        tickets[0] += 1
        copy = pltpu.make_async_remote_copy(
            src_ref=src, dst_ref=dst, send_sem=ss.at[idx], recv_sem=rs.at[idx],
            device_id={axis: peer(axis, j) for axis, j in shifts.items() if j}, device_id_type=MESH,
        )
        copy.start()
        sent.append(copy)
        return idx

    def send(src, dst, axis, j):
        return send_to(src, dst, {axis: j})

    def arrived(idx, dst, axis):
        pltpu.make_async_remote_copy(
            src_ref=dst, dst_ref=dst, send_sem=ss.at[idx], recv_sem=rs.at[idx],
            device_id={axis: peer(axis, 1)}, device_id_type=MESH,
        ).wait_recv()

    def field_send(place):
        hops = [(i, send(place(d, c), place(d, c), "dom", i)) for i in range(1, dom)]
        cross = [(0, k, send(place(d, c), place(d, c), "sub", k)) for k in range(1, sub)]
        return hops, cross

    def field_relay(place, state):
        hops, cross = state
        for i, idx in hops:
            here = place(source("dom", i), c)
            arrived(idx, here, "dom")
            cross += [(i, k, send(here, here, "sub", k)) for k in range(1, sub)]

    def field_done(place, state):
        for i, k, idx in state[1]:
            arrived(idx, place(source("dom", i), source("sub", k)), "sub")

    def slab_send(place, first, second):
        own = place({"shots": s, "dom": d}, c)
        state = {
            "one": [(i, send(own, own, first, i)) for i in range(1, counts[first])],
            "two": [(0, j, send(own, own, second, j)) for j in range(1, counts[second])],
            "cross": [(0, 0, k, send(own, own, "sub", k)) for k in range(1, sub)],
        }
        return state

    def slab_relay(place, state, first, second):
        for i, idx in state["one"]:
            here = place({first: source(first, i), second: me[second]}, c)
            arrived(idx, here, first)
            state["two"] += [(i, j, send(here, here, second, j)) for j in range(1, counts[second])]
            state["cross"] += [(i, 0, k, send(here, here, "sub", k)) for k in range(1, sub)]

    def slab_relay_two(place, state, first, second):
        for i, j, idx in state["two"]:
            here = place({first: source(first, i), second: source(second, j)}, c)
            arrived(idx, here, second)
            state["cross"] += [(i, j, k, send(here, here, "sub", k)) for k in range(1, sub)]

    def slab_done(place, state, first, second):
        for i, j, k, idx in state["cross"]:
            arrived(idx, place({first: source(first, i), second: source(second, j)}, source("sub", k)), "sub")

    def in_field(ref, n):
        return lambda i, k: ref.at[n, :, xs(i), ys(k)]

    def in_whole(ref):
        return lambda i, k: ref.at[:, xs(i), ys(k)]

    def in_slab(ref):
        return lambda at, k: ref.at[pl.ds(at["shots"] * owned, owned), xs(at["dom"]), ys(k)]

    def neighbours(slot, b, exact, lanes=slice(None)):
        lo = b * zb
        acc = None
        for part_of in (0,) if exact else (0, 1):
            near = H[slot, part_of, lo : lo + zb + 2 * reach, :, lanes].reshape((zb + 2 * reach) * X, -1)
            mid = H[slot, part_of, lo + reach : lo + reach + zb].reshape(zb * X, Y)
            term = jnp.dot(zx_ref[...], near, preferred_element_type=F32)
            acc = term if acc is None else acc + term
            acc = acc + jnp.dot(mid, ym_ref[:, lanes], preferred_element_type=F32)
        return acc.reshape(zb, X, -1)

    def keep(slot, z, value, exact=False):
        high = value.astype(BF16)
        H[slot, 0, reach + z] = high
        if not exact:
            H[slot, 1, reach + z] = (value - high.astype(F32)).astype(BF16)

    def amp_at(n):
        return amp_ref[0, n]

    blocks = depth // zb
    barrier = pltpu.get_barrier_semaphore()
    greeted = 0
    for axis, count in counts.items():
        for j in range(1, count):
            pl.semaphore_signal(barrier, inc=1, device_id={axis: peer(axis, j)}, device_id_type=MESH)
            greeted += 1
    for i in range(1, dom):
        for j in range(1, shots):
            pl.semaphore_signal(
                barrier, inc=1, device_id={"shots": peer("shots", j), "dom": peer("dom", i)}, device_id_type=MESH
            )
            greeted += 1

    loads = {}
    for place, source_ref, target in (
        (0, vel_in, vel_ref), (1, now_in, now_ref), (2, sponge_in, sponge_ref), (3, prev_in, prev_ref),
        (4, adj_in, adj_ref), (5, adjn_in, adjn_ref), (6, rec_in, rec_ref), (7, obs_in, obs_ref),
        (8, amp_in, amp_ref), (9, ym_in, ym_ref), (10, zx_in, zx_ref),
    ):
        loads[place] = pltpu.make_async_copy(source_ref, target, ls.at[place])
        loads[place].start()

    own_x, own_y = xs(d), ys(c)
    for z in range(depth):
        PC[z] = jnp.zeros((X, Y), F32)
    loads[0].wait()
    V[pl.ds(s * owned, owned), own_x, own_y] = vel_ref[...]
    loads[1].wait()
    U[1, :, own_x, own_y] = now_ref[0].astype(F32)

    pl.semaphore_wait(barrier, greeted)

    vel_state = slab_send(in_slab(V), "dom", "shots")
    now_state = field_send(in_field(U, 1))
    loads[2].wait()
    SP[:, own_x, own_y] = sponge_ref[...].astype(F32)
    sp_state = field_send(in_whole(SP))
    loads[3].wait()
    U[0, :, own_x, own_y] = prev_ref[0].astype(F32)
    prev_state = field_send(in_field(U, 0))
    loads[4].wait()
    L[1, :, own_x, own_y] = adj_ref[0].astype(F32)
    adj_state = field_send(in_field(L, 1))
    loads[5].wait()
    L[0, :, own_x, own_y] = adjn_ref[0].astype(F32)
    adjn_state = field_send(in_field(L, 0))
    for place in range(6, 11):
        loads[place].wait()

    edge = jnp.zeros((reach, X, Y), BF16)
    for slot in range(H.shape[0]):
        for part_of in range(2):
            H[slot, part_of, 0:reach] = edge
            H[slot, part_of, reach + depth : 2 * reach + depth] = edge
    pos = rec_ref[...]
    row_of = jnp.zeros_like(pos)
    for x in range(1, X):
        row_of = row_of + (pos >= x * Y).astype(jnp.int32)
    col_of = pos - row_of * Y
    nrec = pos.shape[1]
    x_hot = (lax.broadcasted_iota(jnp.int32, (X, nrec), 0) == row_of).astype(F32)
    y_hot = (lax.broadcasted_iota(jnp.int32, (Y, nrec), 0) == col_of).astype(F32).astype(BF16)

    def spread(lhs):
        return lax.dot_general(lhs, y_hot, (((1,), (1,)), ((), ())), preferred_element_type=F32)

    CNT[...] = spread(x_hot.astype(BF16))
    slab_relay(in_slab(V), vel_state, "dom", "shots")
    for n in range(NF):
        vals = x_hot * obs_ref[0, n : n + 1, :]
        a = vals.astype(BF16)
        b, rest = split(vals - a.astype(F32))
        OB[n] = spread(a) + spread(b) + spread(rest)
    flat = lax.broadcasted_iota(jnp.int32, (X, Y), 0) * Y + lax.broadcasted_iota(jnp.int32, (X, Y), 1)
    src_hot = (flat == src_ref[0]).astype(F32)

    field_relay(in_field(U, 1), now_state)
    field_relay(in_whole(SP), sp_state)
    field_done(in_field(U, 1), now_state)
    for z in range(depth):
        keep(0, z, U[1, z], True)
    for b in range(blocks):
        ACC[b * zb : (b + 1) * zb] = neighbours(0, b, True)
    slab_relay_two(in_slab(V), vel_state, "dom", "shots")
    field_relay(in_field(U, 0), prev_state)
    slab_done(in_slab(V), vel_state, "dom", "shots")
    field_done(in_whole(SP), sp_state)
    for z in range(depth):
        inv = 1.0 / (1.0 + damp_rate * SP[z])
        IV[z] = 2.0 * inv
        vel = V[z]
        KP[z] = vel * vel * (unit * inv)
    field_done(in_field(U, 0), prev_state)

    def carried(ref, n, z, xr, yr):
        before = ref[n - 1, z, xr, yr]
        return IV[z, xr, yr] * (ref[n, z, xr, yr] - before) + before

    whole_x, whole_y = slice(None), slice(None)

    def advance(ref, n, slot, plane, at, ready=False):
        for b in range(blocks):
            acc = None if ready else neighbours(slot, b, False)
            for i in range(zb):
                z = b * zb + i
                lap = (ACC[z] if ready else acc[i]) + centre * ref[n, z]
                value = carried(ref, n, z, whole_x, whole_y) + KP[z] * lap
                if z == at:
                    value = value + IV[z] * plane
                ref[n + 1, z] = value
                keep(slot ^ 1, z, value)

    for n in range(NF):
        advance(U, n + 1, n % 2, src_hot * (0.5 * amp_at(n)), src_depth, n == 0)
        if n == max(0, NF - 2):
            field_relay(in_field(L, 1), adj_state)

    for z in range(depth):
        illum = None
        for n in range(NF):
            value = U[n + 2, z, own_x, own_y]
            illum = value * value if illum is None else illum + value * value
        GI[1, z] = illum
    field_done(in_field(L, 1), adj_state)
    for z in range(depth):
        keep(2, z, L[1, z], True)
    for b in range(blocks):
        ACC[b * zb : (b + 1) * zb] = neighbours(2, b, True)
    field_relay(in_field(L, 0), adjn_state)
    far_first = sorted(range(1, shots), key=lambda j: -min(j, shots - j))

    def to_owners(f):
        return [
            (j, send(GI.at[f, pl.ds(peer("shots", j) * owned, owned)], GR.at[j - 1, f], "shots", j))
            for j in far_first
        ]

    illum_parts = to_owners(1)
    field_done(in_field(L, 0), adjn_state)

    def plane_of(n):
        return 0.5 * (CNT[...] * U[n + 1, rec_depth] - OB[n - 1])

    for n in range(NF, 1, -1):
        advance(L, NF + 1 - n, 2 + (NF - n) % 2, plane_of(n), rec_depth, n == NF)

    last = NF
    for b in range(blocks):
        ACC[b * zb : (b + 1) * zb, :, 0:cols] = neighbours(2 + (NF - 1) % 2, b, False, own_y)
    SR[0] = plane_of(1)
    source_plane = SR[0, own_x, own_y]
    for z in range(depth):
        lap = ACC[z, own_x, 0:cols] + centre * L[last, z, own_x, own_y]
        lam = carried(L, last, z, own_x, own_y) + KP[z, own_x, own_y] * lap
        if z == rec_depth:
            lam = lam + IV[z, own_x, own_y] * source_plane
        u = [U[n, z, own_x, own_y] for n in range(NF + 2)]
        grad = lam * (u[2] - 2.0 * u[1] + u[0])
        for n in range(1, NF):
            grad = grad + L[NF + 1 - n, z, own_x, own_y] * (u[n + 2] - 2.0 * u[n + 1] + u[n])
        GI[0, z] = grad

    grad_parts = to_owners(0)
    plane = src_hot * (0.5 * amp_at(NF))
    for b in range(blocks):
        acc = neighbours(NF % 2, b, False)
        for i in range(zb):
            z = b * zb + i
            value = carried(U, NF + 1, z, whole_x, whole_y)
            if z == src_depth:
                value = value + IV[z] * plane
            U[NF + 2, z] = value
            ACC[z] = KP[z] * (acc[i] + centre * U[NF + 1, z])
    below = GI[1, pl.ds(s * owned, owned)] + floor_share * shots
    for j, idx in illum_parts:
        arrived(idx, GR.at[j - 1, 1], "shots")
        below = below + GR[j - 1, 1]
    above = GI[0, pl.ds(s * owned, owned)]
    for j, idx in grad_parts:
        arrived(idx, GR.at[j - 1, 0], "shots")
        above = above + GR[j - 1, 0]
    mine = above / below
    PC[pl.ds(s * owned, owned), own_x, own_y] = mine
    slab = in_slab(PC)
    own = slab(me, c)
    column = [(j, send(own, own, "shots", j)) for j in far_first]
    beside = [
        (i, j, send_to(own, own, {"dom": i, "shots": j})) for i in range(1, dom) for j in far_first + [0]
    ]
    cross = [(0, k, send(own, own, "sub", k)) for k in range(1, sub)]
    for j, idx in reversed(column):
        here = slab({"shots": source("shots", j), "dom": d}, c)
        arrived(idx, here, "shots")
        cross += [(j, k, send(here, here, "sub", k)) for k in range(1, sub)]
    for i, j, idx in reversed(beside):
        arrived(idx, slab({"shots": source("shots", j), "dom": source("dom", i)}, c), "dom")
    top = jnp.abs(PC[0, :, own_y])
    for z in range(1, depth):
        top = jnp.maximum(top, jnp.abs(PC[z, :, own_y]))
    PK[0] = top
    peaks = [(k, send(PK.at[0], PK.at[k], "sub", k)) for k in range(1, sub)]
    for j, k, idx in cross:
        arrived(idx, slab({"shots": source("shots", j), "dom": d}, source("sub", k)), "sub")
    for k, idx in peaks:
        arrived(idx, PK.at[k], "sub")
        top = jnp.maximum(top, PK[k])
    peak = jnp.max(jnp.max(top, axis=0, keepdims=True), axis=1, keepdims=True)
    scale = 1.0 / (peak + 1e-06)
    both_ref[0:owned] = mine * scale
    rate = step_rate * scale
    slot = (NF + 1) % 2
    for z in range(depth):
        factor = 1.0 - rate * PC[z]
        factor = factor * factor
        value = U[NF + 2, z] + ACC[z] * factor
        U[NF + 2, z] = value
        keep(slot, z, value)
    for b in range(blocks):
        ACC[b * zb : (b + 1) * zb, :, 0:cols] = neighbours(slot, b, False, own_y)
    SR[1] = src_hot * (0.5 * amp_at(NF + 1))
    for z in range(depth):
        lap = ACC[z, own_x, 0:cols] + centre * U[NF + 2, z, own_x, own_y]
        factor = 1.0 - rate * PC[z, own_x, own_y]
        value = carried(U, NF + 2, z, own_x, own_y) + KP[z, own_x, own_y] * (factor * factor) * lap
        if z == src_depth:
            value = value + IV[z, own_x, own_y] * SR[1, own_x, own_y]
        both_ref[owned + z] = value
    for copy in sent:
        copy.wait_send()


def part(both_ref, dir_ref, out_ref):
    owned = dir_ref.shape[0]
    dir_ref[...] = both_ref[0:owned]
    out_ref[0] = both_ref[owned:]


def solution(mesh):
    shots, dom, sub = mesh.shape["shots"], mesh.shape["dom"], mesh.shape["sub"]

    def shards(velocity, wave_prev, wave_now, adj_next, adj_now, sponge, wavelet, src_pos, rec_pos, observed):
        depth, rows, cols = sponge.shape
        owned = velocity.shape[0]
        X, Y = dom * rows, sub * cols
        zb = min(depth, max(1, 128 // X))
        ym = along_y(Y)
        zx = along_zx(zb, X)
        vm = pl.BlockSpec(memory_space=pltpu.VMEM)
        hbm = pl.BlockSpec(memory_space=pltpu.HBM)
        sm = pl.BlockSpec(memory_space=pltpu.SMEM)
        operands = (
            velocity, wave_prev, wave_now, adj_next, adj_now, sponge, wavelet, src_pos, rec_pos, observed,
            jnp.asarray(ym), jnp.asarray(zx),
        )
        whole = pltpu.VMEM((depth, X, Y), F32)
        n_sems = copies_needed(shots, dom, sub)
        both = pl.pallas_call(
            functools.partial(kernel, (shots, dom, sub, depth, rows, cols, owned, zb)),
            out_shape=jax.ShapeDtypeStruct((owned + depth, rows, cols), F32),
            in_specs=[sm if a.ndim == 1 else hbm for a in operands],
            out_specs=vm,
            scratch_shapes=[(pltpu.SMEM if a.size < 128 else pltpu.VMEM)(a.shape, a.dtype) for a in operands if a.ndim > 1] + [
                pltpu.VMEM((NF + 3, depth, X, Y), F32),
                pltpu.VMEM((NF + 1, depth, X, Y), F32),
                pltpu.VMEM((4, 2, depth + 2 * reach, X, Y), BF16),
                whole, whole, whole, whole, whole, whole,
                pltpu.VMEM((sub, X, cols), F32),
                pltpu.VMEM((NF, X, Y), F32),
                pltpu.VMEM((X, Y), F32),
                pltpu.VMEM((2, X, Y), F32),
                pltpu.VMEM((2, depth, rows, cols), F32),
                pltpu.VMEM((max(1, shots - 1), 2, owned, rows, cols), F32),
                pltpu.SemaphoreType.DMA((n_sems,)),
                pltpu.SemaphoreType.DMA((n_sems,)),
                pltpu.SemaphoreType.DMA((len(operands) - 1,)),
            ],
            compiler_params=pltpu.CompilerParams(
                collective_id=0, has_side_effects=True, vmem_limit_bytes=VM_MAIN
            ),
        )(*(pltpu.with_memory_space_constraint(a, pltpu.HBM) if a.ndim > 1 else a for a in operands))
        return tuple(pl.pallas_call(
            part,
            out_shape=(
                jax.ShapeDtypeStruct((owned, rows, cols), F32),
                jax.ShapeDtypeStruct((1, depth, rows, cols), F32),
            ),
            in_specs=[vm],
            out_specs=(vm, vm),
            compiler_params=pltpu.CompilerParams(vmem_limit_bytes=VM_PART),
        )(both))

    return jax.shard_map(
        shards,
        mesh=mesh,
        in_specs=(
            P(("groups", "shots"), "dom", "sub"),
            P(("groups", "shots"), None, "dom", "sub"),
            P(("groups", "shots"), None, "dom", "sub"),
            P(("groups", "shots"), None, "dom", "sub"),
            P(("groups", "shots"), None, "dom", "sub"),
            P(None, "dom", "sub"),
            P(("groups", "shots"), None),
            P(("groups", "shots")),
            P(("groups", "shots"), None),
            P(("groups", "shots"), None, None),
        ),
        out_specs=(
            P(("groups", "shots"), "dom", "sub"),
            P(("groups", "shots"), None, "dom", "sub"),
        ),
        check_vma=False,
    )
```

time: 46.3 us -> 42.2 us (0.911)
  Pallas kernels: 44.8 us -> 40.7 us
    pallas_call x1, Pallas kernels: 43.2 us -> 40 us  [shards(): pl.pallas_call(functools.partial(kernel, (shots, dom, sub, depth, rows, c...]
    pallas_call x1, Pallas kernels: 1.59 us -> 0.68 us  [shards(): pl.pallas_call(part, out_shape=(jax.ShapeDtypeStruct((owned, rows, cols),...]
where the time goes in v1:
time: 42.2 us; the launch traced here: 42 us
  Pallas kernels  40.7 us (96%)
  between operations  1.29 us (3%)
    pallas_call x1, Pallas kernels, shards(): pl.pallas_call(functools.partial(kernel, (shots, dom, sub, depth, rows, c...  40 us

profile of v1, /device:TPU:1, one launch (start us, length us, event | category | flops | bytes accessed | tf_op | source)
XLA Modules:
  0.0 42.0 jit_solution(16769906046504512743)
XLA Ops:
  1.3 40.0 %shard_map.131.both_ref = f32[40,8,128]{2,1,0:T(8,128)S(1)} custom-call(f32[8,8,128]{2,1,0:T(8,128)} %vel_in.1, bf16[1,32,8,128]{3,2,1,0:T(8,128)(2,1)} %prev_in.1, bf16[1,32,8,128]{3,2,1,0:T(8,128)(2,1)} %now_in.1, bf16[1,32,8,128]{3,2,1,0:T(8,128)(2,1)} %adjn_in.1, bf16[1,32,8,128]{3,2,1,0:T(8,128)(2,1)} %adj_in.1, s32[32,8,128]{2,1,0:T(8,128)} %sponge_in.1, ...), custom_call_target="tpu_custom_call" | custom-call | tf_op jit(solution)/shard_map/pallas_call | solution.py:443
  41.3 0.7 %shard_map.132 = (f32[8,8,128]{2,1,0:T(8,128)}, f32[1,32,8,128]{3,2,1,0:T(8,128)}) custom-call(f32[40,8,128]{2,1,0:T(8,128)S(1)} %shard_map.131.both_ref), custom_call_target="tpu_custom_call" | custom-call | tf_op jit(solution)/shard_map/pallas_call | solution.py:467

commit v2 on v1

--- a/solution.py
+++ b/solution.py
@@ -56,27 +56,29 @@
     return high, low
 
 
-def copies_needed(shots, dom, sub):
-    fields = 5 * ((dom - 1) + dom * (sub - 1))
+def copies_needed(parts, shots, dom, sub):
+    fields = 4 * ((dom - 1) + dom * (sub - 1))
+    mask = (dom - 1) * (1 + (parts - 1)) + (1 + (dom - 1) * parts) * (sub - 1)
     slab = shots * dom * sub
-    back = (shots * dom - 1) + shots * (sub - 1) + (sub - 1)
-    return fields + slab + 2 * (shots - 1) + back
+    back = (shots - 1) + (dom - 1) * shots * sub + shots * (sub - 1)
+    return fields + mask + slab + 2 * (shots - 1) + back
 
 
 def kernel(
     sizes,
     vel_in, prev_in, now_in, adjn_in, adj_in, sponge_in, amp_in, src_ref, rec_in, obs_in, ym_in, zx_in,
     both_ref,
-    vel_ref, prev_ref, now_ref, adjn_ref, adj_ref, sponge_ref, amp_ref, rec_ref, obs_ref, ym_ref, zx_ref,
-    U, L, H, V, SP, IV, KP, ACC, PC, PK, OB, CNT, SR, GI, GR, ss, rs, ls,
+    prev_ref, now_ref, adjn_ref, adj_ref, amp_ref, rec_ref, obs_ref, ym_ref, zx_ref,
+    U, L, H, V, SP, IV, KP, ACC, PC, HS, HR, CR, OB, CNT, SR, GI, GR, ss, rs, ls,
 ):
-    shots, dom, sub, depth, rows, cols, owned, zb = sizes
+    parts, shots, dom, sub, depth, rows, cols, owned, zb = sizes
     X, Y = dom * rows, sub * cols
     s = lax.axis_index("shots")
     d = lax.axis_index("dom")
     c = lax.axis_index("sub")
-    counts = {"shots": shots, "dom": dom, "sub": sub}
-    me = {"shots": s, "dom": d, "sub": c}
+    g = lax.axis_index("groups") if parts > 1 else 0
+    counts = {"groups": parts, "shots": shots, "dom": dom, "sub": sub}
+    me = {"groups": g, "shots": s, "dom": d, "sub": c}
     tickets = [0]
     sent = []
 
@@ -128,14 +130,13 @@
         for i, k, idx in state[1]:
             arrived(idx, place(source("dom", i), source("sub", k)), "sub")
 
-    def slab_send(place, first, second):
-        own = place({"shots": s, "dom": d}, c)
-        state = {
-            "one": [(i, send(own, own, first, i)) for i in range(1, counts[first])],
-            "two": [(0, j, send(own, own, second, j)) for j in range(1, counts[second])],
-            "cross": [(0, 0, k, send(own, own, "sub", k)) for k in range(1, sub)],
+    def slab_send(place, own, first, second):
+        there = place({"shots": s, "dom": d}, c)
+        return {
+            "one": [(i, send(own, there, first, i)) for i in range(1, counts[first])],
+            "two": [(0, j, send(own, there, second, j)) for j in range(1, counts[second])],
+            "cross": [(0, 0, k, send(own, there, "sub", k)) for k in range(1, sub)],
         }
-        return state
 
     def slab_relay(place, state, first, second):
         for i, idx in state["one"]:
@@ -144,11 +145,12 @@
             state["two"] += [(i, j, send(here, here, second, j)) for j in range(1, counts[second])]
             state["cross"] += [(i, 0, k, send(here, here, "sub", k)) for k in range(1, sub)]
 
-    def slab_relay_two(place, state, first, second):
+    def slab_relay_two(place, state, first, second, which):
         for i, j, idx in state["two"]:
-            here = place({first: source(first, i), second: source(second, j)}, c)
-            arrived(idx, here, second)
-            state["cross"] += [(i, j, k, send(here, here, "sub", k)) for k in range(1, sub)]
+            if (i == 0) == which:
+                here = place({first: source(first, i), second: source(second, j)}, c)
+                arrived(idx, here, second)
+                state["cross"] += [(i, j, k, send(here, here, "sub", k)) for k in range(1, sub)]
 
     def slab_done(place, state, first, second):
         for i, j, k, idx in state["cross"]:
@@ -186,52 +188,60 @@
     blocks = depth // zb
     barrier = pltpu.get_barrier_semaphore()
     greeted = 0
-    for axis, count in counts.items():
-        for j in range(1, count):
-            pl.semaphore_signal(barrier, inc=1, device_id={axis: peer(axis, j)}, device_id_type=MESH)
-            greeted += 1
-    for i in range(1, dom):
-        for j in range(1, shots):
-            pl.semaphore_signal(
-                barrier, inc=1, device_id={"shots": peer("shots", j), "dom": peer("dom", i)}, device_id_type=MESH
-            )
-            greeted += 1
-
-    loads = {}
-    for place, source_ref, target in (
-        (0, vel_in, vel_ref), (1, now_in, now_ref), (2, sponge_in, sponge_ref), (3, prev_in, prev_ref),
-        (4, adj_in, adj_ref), (5, adjn_in, adjn_ref), (6, rec_in, rec_ref), (7, obs_in, obs_ref),
-        (8, amp_in, amp_ref), (9, ym_in, ym_ref), (10, zx_in, zx_ref),
+    shifts = [{"dom": i, "sub": k, "shots": j} for j in range(shots) for i in range(dom) for k in range(sub)][1:]
+    for shift in [{"groups": j} for j in range(1, parts)] + shifts:
+        pl.semaphore_signal(
+            barrier, inc=1, device_id={axis: peer(axis, j) for axis, j in shift.items() if j}, device_id_type=MESH
+        )
+        greeted += 1
+
+    own_x, own_y = xs(d), ys(c)
+    own_slab = in_slab(V)({"shots": s, "dom": d}, c)
+    loads = []
+    for source_ref, target in (
+        (now_in, now_ref), (prev_in, prev_ref), (adj_in, adj_ref), (adjn_in, adjn_ref),
+        (vel_in, own_slab), (sponge_in, SP.at[:, own_x, own_y]),
+        (rec_in, rec_ref), (obs_in, obs_ref), (amp_in, amp_ref), (ym_in, ym_ref), (zx_in, zx_ref),
     ):
-        loads[place] = pltpu.make_async_copy(source_ref, target, ls.at[place])
-        loads[place].start()
-
-    own_x, own_y = xs(d), ys(c)
-    for z in range(depth):
-        PC[z] = jnp.zeros((X, Y), F32)
+        loads.append(pltpu.make_async_copy(source_ref, target, ls.at[len(loads)]))
+        loads[-1].start()
     loads[0].wait()
-    V[pl.ds(s * owned, owned), own_x, own_y] = vel_ref[...]
+    U[1, :, own_x, own_y] = now_ref[0].astype(F32)
+
+    pl.semaphore_wait(barrier, greeted)
+
+    share = depth // parts
+
+    def piece(part_at):
+        return pl.ds(pl.multiple_of(part_at * share, share), share)
+
+    vel_state = slab_send(in_slab(V), vel_in, "dom", "shots")
+    mask_state = [(i, send(sponge_in.at[piece(g)], SP.at[piece(g), own_x, own_y], "dom", i)) for i in range(1, dom)]
+    now_state = field_send(in_field(U, 1))
+    mask_cross = [
+        (SP.at[:, own_x, ys(source("sub", k))], send(sponge_in, SP.at[:, own_x, own_y], "sub", k)) for k in range(1, sub)
+    ]
     loads[1].wait()
-    U[1, :, own_x, own_y] = now_ref[0].astype(F32)
-
-    pl.semaphore_wait(barrier, greeted)
-
-    vel_state = slab_send(in_slab(V), "dom", "shots")
-    now_state = field_send(in_field(U, 1))
-    loads[2].wait()
-    SP[:, own_x, own_y] = sponge_ref[...].astype(F32)
-    sp_state = field_send(in_whole(SP))
-    loads[3].wait()
     U[0, :, own_x, own_y] = prev_ref[0].astype(F32)
     prev_state = field_send(in_field(U, 0))
-    loads[4].wait()
+    loads[2].wait()
     L[1, :, own_x, own_y] = adj_ref[0].astype(F32)
     adj_state = field_send(in_field(L, 1))
-    loads[5].wait()
+    loads[3].wait()
     L[0, :, own_x, own_y] = adjn_ref[0].astype(F32)
     adjn_state = field_send(in_field(L, 0))
-    for place in range(6, 11):
-        loads[place].wait()
+    for z in range(depth):
+        PC[z] = jnp.zeros((X, Y), F32)
+    for load in loads[4:]:
+        load.wait()
+
+    def mask_pass(part_at, i, idx, axis):
+        there = xs(source("dom", i))
+        here = SP.at[piece(part_at), there, own_y]
+        arrived(idx, here, axis)
+        for k in range(1, sub):
+            mask_cross.append((SP.at[piece(part_at), there, ys(source("sub", k))], send(here, here, "sub", k)))
+        return here
 
     edge = jnp.zeros((reach, X, Y), BF16)
     for slot in range(H.shape[0]):
@@ -252,6 +262,11 @@
 
     CNT[...] = spread(x_hot.astype(BF16))
     slab_relay(in_slab(V), vel_state, "dom", "shots")
+    mask_far = []
+    for i, idx in mask_state:
+        here = mask_pass(g, i, idx, "dom")
+        mask_far += [(i, j, send(here, here, "groups", j)) for j in range(1, parts)]
+    slab_relay_two(in_slab(V), vel_state, "dom", "shots", True)
     for n in range(NF):
         vals = x_hot * obs_ref[0, n : n + 1, :]
         a = vals.astype(BF16)
@@ -261,21 +276,23 @@
     src_hot = (flat == src_ref[0]).astype(F32)
 
     field_relay(in_field(U, 1), now_state)
-    field_relay(in_whole(SP), sp_state)
     field_done(in_field(U, 1), now_state)
     for z in range(depth):
         keep(0, z, U[1, z], True)
     for b in range(blocks):
         ACC[b * zb : (b + 1) * zb] = neighbours(0, b, True)
-    slab_relay_two(in_slab(V), vel_state, "dom", "shots")
+    slab_relay_two(in_slab(V), vel_state, "dom", "shots", False)
+    for i, j, idx in mask_far:
+        mask_pass(source("groups", j), i, idx, "groups")
     field_relay(in_field(U, 0), prev_state)
     slab_done(in_slab(V), vel_state, "dom", "shots")
-    field_done(in_whole(SP), sp_state)
-    for z in range(depth):
-        inv = 1.0 / (1.0 + damp_rate * SP[z])
-        IV[z] = 2.0 * inv
+    for here, idx in mask_cross:
+        arrived(idx, here, "sub")
+    for z in range(depth):
+        twice = 2.0 - (2.0 - 2.0 / (1.0 + damp_rate)) * SP[z].astype(F32)
+        IV[z] = twice
         vel = V[z]
-        KP[z] = vel * vel * (unit * inv)
+        KP[z] = vel * vel * (0.5 * unit * twice)
     field_done(in_field(U, 0), prev_state)
 
     def carried(ref, n, z, xr, yr):
@@ -369,27 +386,51 @@
     PC[pl.ds(s * owned, owned), own_x, own_y] = mine
     slab = in_slab(PC)
     own = slab(me, c)
-    column = [(j, send(own, own, "shots", j)) for j in far_first]
-    beside = [
-        (i, j, send_to(own, own, {"dom": i, "shots": j})) for i in range(1, dom) for j in far_first + [0]
-    ]
+    most = jnp.max(jnp.abs(mine), axis=0)
+    most = functools.reduce(jnp.maximum, [most[r : r + reach] for r in range(0, rows, reach)])
+    for i in range(1, dom):
+        HS[i - 1, 0:owned] = jnp.where(peer("dom", i) > d, mine[:, rows - reach : rows], mine[:, 0:reach])
+        HS[i - 1, owned] = most
+    column, beside, corner = [], [], []
+    for j in far_first + [0]:
+        if j:
+            column.append((j, send(own, own, "shots", j)))
+        for i in range(1, dom):
+            beside.append((i, j, send_to(HS.at[i - 1], HR.at[i - 1, s], {"dom": i, "shots": j})))
+            for k in range(1, sub):
+                corner.append((
+                    i, j, k,
+                    send_to(HS.at[i - 1, owned], CR.at[i - 1, k - 1, s], {"dom": i, "shots": j, "sub": k}),
+                ))
     cross = [(0, k, send(own, own, "sub", k)) for k in range(1, sub)]
     for j, idx in reversed(column):
         here = slab({"shots": source("shots", j), "dom": d}, c)
         arrived(idx, here, "shots")
         cross += [(j, k, send(here, here, "sub", k)) for k in range(1, sub)]
+    top = jnp.abs(PC[0, own_x, own_y])
+    for z in range(1, depth):
+        top = jnp.maximum(top, jnp.abs(PC[z, own_x, own_y]))
+    for i, j, k, idx in reversed(corner):
+        arrived(idx, CR.at[i - 1, k - 1, source("shots", j)], "dom")
     for i, j, idx in reversed(beside):
-        arrived(idx, slab({"shots": source("shots", j), "dom": source("dom", i)}, c), "dom")
-    top = jnp.abs(PC[0, :, own_y])
-    for z in range(1, depth):
-        top = jnp.maximum(top, jnp.abs(PC[z, :, own_y]))
-    PK[0] = top
-    peaks = [(k, send(PK.at[0], PK.at[k], "sub", k)) for k in range(1, sub)]
+        arrived(idx, HR.at[i - 1, source("shots", j)], "dom")
+    rest = None
+    for i in range(1, dom):
+        across = xs(source("dom", i))
+        for z in range(depth):
+            halo = HR[i - 1, z // owned, z % owned]
+            PC[z, across, own_y] = jnp.concatenate([halo] * (rows // reach), axis=0)
+        for j in range(shots):
+            values = [HR[i - 1, j, owned]] + [CR[i - 1, k - 1, j] for k in range(1, sub)]
+            for value in values:
+                rest = value if rest is None else jnp.maximum(rest, value)
     for j, k, idx in cross:
         arrived(idx, slab({"shots": source("shots", j), "dom": d}, source("sub", k)), "sub")
-    for k, idx in peaks:
-        arrived(idx, PK.at[k], "sub")
-        top = jnp.maximum(top, PK[k])
+    for k in range(1, sub):
+        for z in range(depth):
+            top = jnp.maximum(top, jnp.abs(PC[z, own_x, ys(source("sub", k))]))
+    if rest is not None:
+        top = jnp.concatenate([top, rest], axis=0)
     peak = jnp.max(jnp.max(top, axis=0, keepdims=True), axis=1, keepdims=True)
     scale = 1.0 / (peak + 1e-06)
     both_ref[0:owned] = mine * scale
@@ -423,6 +464,7 @@
 
 def solution(mesh):
     shots, dom, sub = mesh.shape["shots"], mesh.shape["dom"], mesh.shape["sub"]
+    parts = mesh.shape["groups"]
 
     def shards(velocity, wave_prev, wave_now, adj_next, adj_now, sponge, wavelet, src_pos, rec_pos, observed):
         depth, rows, cols = sponge.shape
@@ -439,18 +481,24 @@
             jnp.asarray(ym), jnp.asarray(zx),
         )
         whole = pltpu.VMEM((depth, X, Y), F32)
-        n_sems = copies_needed(shots, dom, sub)
+        share = parts if depth % parts == 0 else 1
+        n_sems = copies_needed(share, shots, dom, sub)
         both = pl.pallas_call(
-            functools.partial(kernel, (shots, dom, sub, depth, rows, cols, owned, zb)),
+            functools.partial(kernel, (share, shots, dom, sub, depth, rows, cols, owned, zb)),
             out_shape=jax.ShapeDtypeStruct((owned + depth, rows, cols), F32),
             in_specs=[sm if a.ndim == 1 else hbm for a in operands],
             out_specs=vm,
-            scratch_shapes=[(pltpu.SMEM if a.size < 128 else pltpu.VMEM)(a.shape, a.dtype) for a in operands if a.ndim > 1] + [
+            scratch_shapes=[
+                (pltpu.SMEM if a.size < 128 else pltpu.VMEM)(a.shape, a.dtype)
+                for a in operands if a.ndim > 1 and a is not velocity and a is not sponge
+            ] + [
                 pltpu.VMEM((NF + 3, depth, X, Y), F32),
                 pltpu.VMEM((NF + 1, depth, X, Y), F32),
                 pltpu.VMEM((4, 2, depth + 2 * reach, X, Y), BF16),
-                whole, whole, whole, whole, whole, whole,
-                pltpu.VMEM((sub, X, cols), F32),
+                whole, pltpu.VMEM((depth, X, Y), jnp.int32), whole, whole, whole, whole,
+                pltpu.VMEM((max(1, dom - 1), owned + 1, reach, cols), F32),
+                pltpu.VMEM((max(1, dom - 1), shots, owned + 1, reach, cols), F32),
+                pltpu.VMEM((max(1, dom - 1), max(1, sub - 1), shots, reach, cols), F32),
                 pltpu.VMEM((NF, X, Y), F32),
                 pltpu.VMEM((X, Y), F32),
                 pltpu.VMEM((2, X, Y), F32),

time: 42.2 us -> 38.8 us (0.919)
  Pallas kernels: 40.7 us -> 37 us
    pallas_call x1, Pallas kernels: 40 us -> 36.3 us  [shards(): pl.pallas_call(functools.partial(kernel, (share, shots, dom, sub, depth,...]
where the time goes in v2:
time: 38.8 us; the launch traced here: 38.3 us
  Pallas kernels  37 us (95%)
  between operations  1.29 us (3%)
    pallas_call x1, Pallas kernels, shards(): pl.pallas_call(functools.partial(kernel, (share, shots, dom, sub, depth,...  36.3 us

profile of v2, /device:TPU:1, one launch (start us, length us, event | category | flops | bytes accessed | tf_op | source)
XLA Modules:
  0.0 38.3 jit_solution(927521278215136422)
XLA Ops:
  1.3 36.3 %shard_map.131.both_ref = f32[40,8,128]{2,1,0:T(8,128)S(1)} custom-call(f32[8,8,128]{2,1,0:T(8,128)} %vel_in.1, bf16[1,32,8,128]{3,2,1,0:T(8,128)(2,1)} %prev_in.1, bf16[1,32,8,128]{3,2,1,0:T(8,128)(2,1)} %now_in.1, bf16[1,32,8,128]{3,2,1,0:T(8,128)(2,1)} %adjn_in.1, bf16[1,32,8,128]{3,2,1,0:T(8,128)(2,1)} %adj_in.1, s32[32,8,128]{2,1,0:T(8,128)} %sponge_in.1, ...), custom_call_target="tpu_custom_call" | custom-call | tf_op jit(solution)/shard_map/pallas_call | solution.py:486
  37.6 0.7 %shard_map.132 = (f32[8,8,128]{2,1,0:T(8,128)}, f32[1,32,8,128]{3,2,1,0:T(8,128)}) custom-call(f32[40,8,128]{2,1,0:T(8,128)S(1)} %shard_map.131.both_ref), custom_call_target="tpu_custom_call" | custom-call | tf_op jit(solution)/shard_map/pallas_call | solution.py:515

commit v3 on v2

--- a/solution.py
+++ b/solution.py
@@ -56,12 +56,7 @@
     return high, low
 
 
-def copies_needed(parts, shots, dom, sub):
-    fields = 4 * ((dom - 1) + dom * (sub - 1))
-    mask = (dom - 1) * (1 + (parts - 1)) + (1 + (dom - 1) * parts) * (sub - 1)
-    slab = shots * dom * sub
-    back = (shots - 1) + (dom - 1) * shots * sub + shots * (sub - 1)
-    return fields + mask + slab + 2 * (shots - 1) + back
+N_SEMS = 22
 
 
 def kernel(
@@ -71,16 +66,15 @@
     prev_ref, now_ref, adjn_ref, adj_ref, amp_ref, rec_ref, obs_ref, ym_ref, zx_ref,
     U, L, H, V, SP, IV, KP, ACC, PC, HS, HR, CR, OB, CNT, SR, GI, GR, ss, rs, ls,
 ):
-    parts, shots, dom, sub, depth, rows, cols, owned, zb = sizes
+    parts, shots, dom, sub, depth, rows, cols, owned, zb, sharing = sizes
     X, Y = dom * rows, sub * cols
     s = lax.axis_index("shots")
     d = lax.axis_index("dom")
     c = lax.axis_index("sub")
-    g = lax.axis_index("groups") if parts > 1 else 0
+    g = lax.axis_index("groups")
     counts = {"groups": parts, "shots": shots, "dom": dom, "sub": sub}
     me = {"groups": g, "shots": s, "dom": d, "sub": c}
-    tickets = [0]
-    sent = []
+    groups = []
 
     def peer(axis, j):
         return lax.rem(me[axis] + j, counts[axis])
@@ -94,73 +88,44 @@
     def ys(i):
         return pl.ds(pl.multiple_of(i * cols, cols), cols)
 
-    def send_to(src, dst, shifts):
-        idx = tickets[0]
-        tickets[0] += 1
-        copy = pltpu.make_async_remote_copy(
+    def group(total):
+        groups.append(total)
+        return len(groups) - 1
+
+    def put(idx, src, dst, shifts):
+        pltpu.make_async_remote_copy(
             src_ref=src, dst_ref=dst, send_sem=ss.at[idx], recv_sem=rs.at[idx],
             device_id={axis: peer(axis, j) for axis, j in shifts.items() if j}, device_id_type=MESH,
+        ).start()
+
+    def whole_group(idx):
+        return pltpu.make_async_remote_copy(
+            src_ref=groups[idx], dst_ref=groups[idx], send_sem=ss.at[idx], recv_sem=rs.at[idx],
+            device_id={"sub": peer("sub", 1)}, device_id_type=MESH,
         )
-        copy.start()
-        sent.append(copy)
-        return idx
-
-    def send(src, dst, axis, j):
-        return send_to(src, dst, {axis: j})
-
-    def arrived(idx, dst, axis):
-        pltpu.make_async_remote_copy(
-            src_ref=dst, dst_ref=dst, send_sem=ss.at[idx], recv_sem=rs.at[idx],
-            device_id={axis: peer(axis, 1)}, device_id_type=MESH,
-        ).wait_recv()
-
-    def field_send(place):
-        hops = [(i, send(place(d, c), place(d, c), "dom", i)) for i in range(1, dom)]
-        cross = [(0, k, send(place(d, c), place(d, c), "sub", k)) for k in range(1, sub)]
-        return hops, cross
-
-    def field_relay(place, state):
-        hops, cross = state
-        for i, idx in hops:
-            here = place(source("dom", i), c)
-            arrived(idx, here, "dom")
-            cross += [(i, k, send(here, here, "sub", k)) for k in range(1, sub)]
-
-    def field_done(place, state):
-        for i, k, idx in state[1]:
-            arrived(idx, place(source("dom", i), source("sub", k)), "sub")
-
-    def slab_send(place, own, first, second):
-        there = place({"shots": s, "dom": d}, c)
-        return {
-            "one": [(i, send(own, there, first, i)) for i in range(1, counts[first])],
-            "two": [(0, j, send(own, there, second, j)) for j in range(1, counts[second])],
-            "cross": [(0, 0, k, send(own, there, "sub", k)) for k in range(1, sub)],
-        }
-
-    def slab_relay(place, state, first, second):
-        for i, idx in state["one"]:
-            here = place({first: source(first, i), second: me[second]}, c)
-            arrived(idx, here, first)
-            state["two"] += [(i, j, send(here, here, second, j)) for j in range(1, counts[second])]
-            state["cross"] += [(i, 0, k, send(here, here, "sub", k)) for k in range(1, sub)]
-
-    def slab_relay_two(place, state, first, second, which):
-        for i, j, idx in state["two"]:
-            if (i == 0) == which:
-                here = place({first: source(first, i), second: source(second, j)}, c)
-                arrived(idx, here, second)
-                state["cross"] += [(i, j, k, send(here, here, "sub", k)) for k in range(1, sub)]
-
-    def slab_done(place, state, first, second):
-        for i, j, k, idx in state["cross"]:
-            arrived(idx, place({first: source(first, i), second: source(second, j)}, source("sub", k)), "sub")
-
-    def in_field(ref, n):
-        return lambda i, k: ref.at[n, :, xs(i), ys(k)]
-
-    def in_whole(ref):
-        return lambda i, k: ref.at[:, xs(i), ys(k)]
+
+    def take(idx):
+        whole_group(idx).wait_recv()
+
+    def put_sub(idx, src, dst):
+        for k in range(1, sub):
+            put(idx, src, dst, {"sub": k})
+
+    far_cols, far_rows = pl.ds(0, (sub - 1) * cols), pl.ds(0, (dom - 1) * rows)
+
+    def field_send(ref, n):
+        state = group(ref.at[n, :, far_rows, 0:cols]), group(ref.at[n, :, :, far_cols])
+        here = ref.at[n, :, xs(d), ys(c)]
+        for i in range(1, dom):
+            put(state[0], here, here, {"dom": i})
+        put_sub(state[1], here, here)
+        return state
+
+    def field_relay(ref, n, state):
+        take(state[0])
+        for i in range(1, dom):
+            here = ref.at[n, :, xs(source("dom", i)), ys(c)]
+            put_sub(state[1], here, here)
 
     def in_slab(ref):
         return lambda at, k: ref.at[pl.ds(at["shots"] * owned, owned), xs(at["dom"]), ys(k)]
@@ -188,8 +153,9 @@
     blocks = depth // zb
     barrier = pltpu.get_barrier_semaphore()
     greeted = 0
-    shifts = [{"dom": i, "sub": k, "shots": j} for j in range(shots) for i in range(dom) for k in range(sub)][1:]
-    for shift in [{"groups": j} for j in range(1, parts)] + shifts:
+    shifts = [{"shots": j, "dom": i, "sub": k} for j in range(shots) for i in range(dom) for k in range(sub)][1:]
+    sharers = [{"groups": i, "shots": j} for j in range(shots) for i in range(parts if sharing > shots else 1)][1:sharing]
+    for shift in [shift for shift in sharers if shift["groups"]] + shifts:
         pl.semaphore_signal(
             barrier, inc=1, device_id={axis: peer(axis, j) for axis, j in shift.items() if j}, device_id_type=MESH
         )
@@ -205,43 +171,42 @@
     ):
         loads.append(pltpu.make_async_copy(source_ref, target, ls.at[len(loads)]))
         loads[-1].start()
+
+    pl.semaphore_wait(barrier, greeted)
+
+    share = depth // sharing
+    mine_at = pl.ds(pl.multiple_of((g * shots + s if sharing > shots else s) * share, share), share) if sharing > 1 else slice(None)
+    slab = in_slab(V)
+    vel_across = group(V.at[0:owned, far_rows, 0:cols])
+    vel_near = group(V.at[pl.ds(0, (shots - 1) * owned), 0:rows, 0:cols])
+    vel_far = group(V.at[pl.ds(0, (shots - 1) * owned), far_rows, 0:cols])
+    vel_cross = group(V.at[:, :, far_cols])
+    mask_across = group(SP.at[0:share, far_rows, 0:cols])
+    mask_far = group(SP.at[pl.ds(0, (sharing - 1) * share), far_rows, 0:cols]) if sharing > 1 else None
+    mask_cross = group(SP.at[:, :, far_cols])
+    for i in range(1, dom):
+        put(vel_across, vel_in, own_slab, {"dom": i})
+        put(mask_across, sponge_in.at[mine_at], SP.at[mine_at, own_x, own_y], {"dom": i})
+    for j in range(1, shots):
+        put(vel_near, vel_in, own_slab, {"shots": j})
     loads[0].wait()
     U[1, :, own_x, own_y] = now_ref[0].astype(F32)
-
-    pl.semaphore_wait(barrier, greeted)
-
-    share = depth // parts
-
-    def piece(part_at):
-        return pl.ds(pl.multiple_of(part_at * share, share), share)
-
-    vel_state = slab_send(in_slab(V), vel_in, "dom", "shots")
-    mask_state = [(i, send(sponge_in.at[piece(g)], SP.at[piece(g), own_x, own_y], "dom", i)) for i in range(1, dom)]
-    now_state = field_send(in_field(U, 1))
-    mask_cross = [
-        (SP.at[:, own_x, ys(source("sub", k))], send(sponge_in, SP.at[:, own_x, own_y], "sub", k)) for k in range(1, sub)
-    ]
+    now_state = field_send(U, 1)
+    put_sub(vel_cross, vel_in, own_slab)
+    put_sub(mask_cross, sponge_in, SP.at[:, own_x, own_y])
     loads[1].wait()
     U[0, :, own_x, own_y] = prev_ref[0].astype(F32)
-    prev_state = field_send(in_field(U, 0))
+    prev_state = field_send(U, 0)
     loads[2].wait()
     L[1, :, own_x, own_y] = adj_ref[0].astype(F32)
-    adj_state = field_send(in_field(L, 1))
+    adj_state = field_send(L, 1)
     loads[3].wait()
     L[0, :, own_x, own_y] = adjn_ref[0].astype(F32)
-    adjn_state = field_send(in_field(L, 0))
+    adjn_state = field_send(L, 0)
     for z in range(depth):
         PC[z] = jnp.zeros((X, Y), F32)
     for load in loads[4:]:
         load.wait()
-
-    def mask_pass(part_at, i, idx, axis):
-        there = xs(source("dom", i))
-        here = SP.at[piece(part_at), there, own_y]
-        arrived(idx, here, axis)
-        for k in range(1, sub):
-            mask_cross.append((SP.at[piece(part_at), there, ys(source("sub", k))], send(here, here, "sub", k)))
-        return here
 
     edge = jnp.zeros((reach, X, Y), BF16)
     for slot in range(H.shape[0]):
@@ -261,12 +226,21 @@
         return lax.dot_general(lhs, y_hot, (((1,), (1,)), ((), ())), preferred_element_type=F32)
 
     CNT[...] = spread(x_hot.astype(BF16))
-    slab_relay(in_slab(V), vel_state, "dom", "shots")
-    mask_far = []
-    for i, idx in mask_state:
-        here = mask_pass(g, i, idx, "dom")
-        mask_far += [(i, j, send(here, here, "groups", j)) for j in range(1, parts)]
-    slab_relay_two(in_slab(V), vel_state, "dom", "shots", True)
+    take(vel_across)
+    for i in range(1, dom):
+        here = slab({"shots": s, "dom": source("dom", i)}, c)
+        for j in range(1, shots):
+            put(vel_far, here, here, {"shots": j})
+        put_sub(vel_cross, here, here)
+    take(mask_across)
+    for i in range(1, dom):
+        here = SP.at[mine_at, xs(source("dom", i)), own_y]
+        for shift in sharers:
+            put(mask_far, here, here, shift)
+    take(vel_near)
+    for j in range(1, shots):
+        here = slab({"shots": source("shots", j), "dom": d}, c)
+        put_sub(vel_cross, here, here)
     for n in range(NF):
         vals = x_hot * obs_ref[0, n : n + 1, :]
         a = vals.astype(BF16)
@@ -275,25 +249,31 @@
     flat = lax.broadcasted_iota(jnp.int32, (X, Y), 0) * Y + lax.broadcasted_iota(jnp.int32, (X, Y), 1)
     src_hot = (flat == src_ref[0]).astype(F32)
 
-    field_relay(in_field(U, 1), now_state)
-    field_done(in_field(U, 1), now_state)
+    field_relay(U, 1, now_state)
+    take(now_state[1])
     for z in range(depth):
         keep(0, z, U[1, z], True)
     for b in range(blocks):
         ACC[b * zb : (b + 1) * zb] = neighbours(0, b, True)
-    slab_relay_two(in_slab(V), vel_state, "dom", "shots", False)
-    for i, j, idx in mask_far:
-        mask_pass(source("groups", j), i, idx, "groups")
-    field_relay(in_field(U, 0), prev_state)
-    slab_done(in_slab(V), vel_state, "dom", "shots")
-    for here, idx in mask_cross:
-        arrived(idx, here, "sub")
+    take(vel_far)
+    for i in range(1, dom):
+        for j in range(1, shots):
+            here = slab({"shots": source("shots", j), "dom": source("dom", i)}, c)
+            put_sub(vel_cross, here, here)
+    field_relay(U, 0, prev_state)
+    if sharing > 1:
+        take(mask_far)
+    for i in range(1, dom):
+        here = SP.at[:, xs(source("dom", i)), own_y]
+        put_sub(mask_cross, here, here)
+    take(vel_cross)
+    take(mask_cross)
     for z in range(depth):
         twice = 2.0 - (2.0 - 2.0 / (1.0 + damp_rate)) * SP[z].astype(F32)
         IV[z] = twice
         vel = V[z]
         KP[z] = vel * vel * (0.5 * unit * twice)
-    field_done(in_field(U, 0), prev_state)
+    take(prev_state[1])
 
     def carried(ref, n, z, xr, yr):
         before = ref[n - 1, z, xr, yr]
@@ -316,7 +296,7 @@
     for n in range(NF):
         advance(U, n + 1, n % 2, src_hot * (0.5 * amp_at(n)), src_depth, n == 0)
         if n == max(0, NF - 2):
-            field_relay(in_field(L, 1), adj_state)
+            field_relay(L, 1, adj_state)
 
     for z in range(depth):
         illum = None
@@ -324,22 +304,22 @@
             value = U[n + 2, z, own_x, own_y]
             illum = value * value if illum is None else illum + value * value
         GI[1, z] = illum
-    field_done(in_field(L, 1), adj_state)
+    take(adj_state[1])
     for z in range(depth):
         keep(2, z, L[1, z], True)
     for b in range(blocks):
         ACC[b * zb : (b + 1) * zb] = neighbours(2, b, True)
-    field_relay(in_field(L, 0), adjn_state)
+    field_relay(L, 0, adjn_state)
     far_first = sorted(range(1, shots), key=lambda j: -min(j, shots - j))
 
     def to_owners(f):
-        return [
-            (j, send(GI.at[f, pl.ds(peer("shots", j) * owned, owned)], GR.at[j - 1, f], "shots", j))
-            for j in far_first
-        ]
+        idx = group(GR.at[f])
+        for j in far_first:
+            put(idx, GI.at[f, pl.ds(peer("shots", j) * owned, owned)], GR.at[f, j - 1], {"shots": j})
+        return idx
 
     illum_parts = to_owners(1)
-    field_done(in_field(L, 0), adjn_state)
+    take(adjn_state[1])
 
     def plane_of(n):
         return 0.5 * (CNT[...] * U[n + 1, rec_depth] - OB[n - 1])
@@ -375,13 +355,13 @@
             U[NF + 2, z] = value
             ACC[z] = KP[z] * (acc[i] + centre * U[NF + 1, z])
     below = GI[1, pl.ds(s * owned, owned)] + floor_share * shots
-    for j, idx in illum_parts:
-        arrived(idx, GR.at[j - 1, 1], "shots")
-        below = below + GR[j - 1, 1]
+    take(illum_parts)
+    for j in range(1, shots):
+        below = below + GR[1, j - 1]
     above = GI[0, pl.ds(s * owned, owned)]
-    for j, idx in grad_parts:
-        arrived(idx, GR.at[j - 1, 0], "shots")
-        above = above + GR[j - 1, 0]
+    take(grad_parts)
+    for j in range(1, shots):
+        above = above + GR[0, j - 1]
     mine = above / below
     PC[pl.ds(s * owned, owned), own_x, own_y] = mine
     slab = in_slab(PC)
@@ -391,46 +371,47 @@
     for i in range(1, dom):
         HS[i - 1, 0:owned] = jnp.where(peer("dom", i) > d, mine[:, rows - reach : rows], mine[:, 0:reach])
         HS[i - 1, owned] = most
-    column, beside, corner = [], [], []
+    close = [j for j in range(1, shots) if min(j, shots - j) == 1]
+    column = {}
+    for members in (close, [j for j in far_first if j not in close]):
+        if members:
+            idx = group(PC.at[pl.ds(0, len(members) * owned), 0:rows, 0:cols])
+            column[idx] = members
+    which = {j: idx for idx, members in column.items() for j in members}
+    beside, corner, cross = group(HR), group(CR), group(PC.at[:, 0:rows, far_cols])
     for j in far_first + [0]:
         if j:
-            column.append((j, send(own, own, "shots", j)))
+            put(which[j], own, own, {"shots": j})
         for i in range(1, dom):
-            beside.append((i, j, send_to(HS.at[i - 1], HR.at[i - 1, s], {"dom": i, "shots": j})))
+            put(beside, HS.at[i - 1], HR.at[i - 1, s], {"dom": i, "shots": j})
             for k in range(1, sub):
-                corner.append((
-                    i, j, k,
-                    send_to(HS.at[i - 1, owned], CR.at[i - 1, k - 1, s], {"dom": i, "shots": j, "sub": k}),
-                ))
-    cross = [(0, k, send(own, own, "sub", k)) for k in range(1, sub)]
-    for j, idx in reversed(column):
-        here = slab({"shots": source("shots", j), "dom": d}, c)
-        arrived(idx, here, "shots")
-        cross += [(j, k, send(here, here, "sub", k)) for k in range(1, sub)]
+                put(corner, HS.at[i - 1, owned], CR.at[i - 1, k - 1, s], {"dom": i, "shots": j, "sub": k})
+    put_sub(cross, own, own)
+    for idx, members in column.items():
+        take(idx)
+        for j in members:
+            here = slab({"shots": source("shots", j), "dom": d}, c)
+            put_sub(cross, here, here)
     top = jnp.abs(PC[0, own_x, own_y])
     for z in range(1, depth):
         top = jnp.maximum(top, jnp.abs(PC[z, own_x, own_y]))
-    for i, j, k, idx in reversed(corner):
-        arrived(idx, CR.at[i - 1, k - 1, source("shots", j)], "dom")
-    for i, j, idx in reversed(beside):
-        arrived(idx, HR.at[i - 1, source("shots", j)], "dom")
+    take(cross)
+    for k in range(1, sub):
+        for z in range(depth):
+            top = jnp.maximum(top, jnp.abs(PC[z, own_x, ys(source("sub", k))]))
+    take(corner)
+    take(beside)
     rest = None
     for i in range(1, dom):
         across = xs(source("dom", i))
-        for z in range(depth):
-            halo = HR[i - 1, z // owned, z % owned]
-            PC[z, across, own_y] = jnp.concatenate([halo] * (rows // reach), axis=0)
         for j in range(shots):
             values = [HR[i - 1, j, owned]] + [CR[i - 1, k - 1, j] for k in range(1, sub)]
             for value in values:
                 rest = value if rest is None else jnp.maximum(rest, value)
-    for j, k, idx in cross:
-        arrived(idx, slab({"shots": source("shots", j), "dom": d}, source("sub", k)), "sub")
-    for k in range(1, sub):
         for z in range(depth):
-            top = jnp.maximum(top, jnp.abs(PC[z, own_x, ys(source("sub", k))]))
-    if rest is not None:
-        top = jnp.concatenate([top, rest], axis=0)
+            halo = HR[i - 1, z // owned, z % owned]
+            PC[z, across, own_y] = jnp.concatenate([halo] * (rows // reach), axis=0)
+    top = jnp.concatenate([top, rest], axis=0)
     peak = jnp.max(jnp.max(top, axis=0, keepdims=True), axis=1, keepdims=True)
     scale = 1.0 / (peak + 1e-06)
     both_ref[0:owned] = mine * scale
@@ -452,8 +433,8 @@
         if z == src_depth:
             value = value + IV[z, own_x, own_y] * SR[1, own_x, own_y]
         both_ref[owned + z] = value
-    for copy in sent:
-        copy.wait_send()
+    for idx in range(len(groups)):
+        whole_group(idx).wait_send()
 
 
 def part(both_ref, dir_ref, out_ref):
@@ -481,10 +462,9 @@
             jnp.asarray(ym), jnp.asarray(zx),
         )
         whole = pltpu.VMEM((depth, X, Y), F32)
-        share = parts if depth % parts == 0 else 1
-        n_sems = copies_needed(share, shots, dom, sub)
+        sharing = max([n for n in (parts * shots, shots) if depth % n == 0], default=1)
         both = pl.pallas_call(
-            functools.partial(kernel, (share, shots, dom, sub, depth, rows, cols, owned, zb)),
+            functools.partial(kernel, (parts, shots, dom, sub, depth, rows, cols, owned, zb, sharing)),
             out_shape=jax.ShapeDtypeStruct((owned + depth, rows, cols), F32),
             in_specs=[sm if a.ndim == 1 else hbm for a in operands],
             out_specs=vm,
@@ -503,9 +483,9 @@
                 pltpu.VMEM((X, Y), F32),
                 pltpu.VMEM((2, X, Y), F32),
                 pltpu.VMEM((2, depth, rows, cols), F32),
-                pltpu.VMEM((max(1, shots - 1), 2, owned, rows, cols), F32),
-                pltpu.SemaphoreType.DMA((n_sems,)),
-                pltpu.SemaphoreType.DMA((n_sems,)),
+                pltpu.VMEM((2, max(1, shots - 1), owned, rows, cols), F32),
+                pltpu.SemaphoreType.DMA((N_SEMS,)),
+                pltpu.SemaphoreType.DMA((N_SEMS,)),
                 pltpu.SemaphoreType.DMA((len(operands) - 1,)),
             ],
             compiler_params=pltpu.CompilerParams(

time: 38.8 us -> 37.9 us (0.977)
  Pallas kernels: 37 us -> 36.4 us
    pallas_call x1, Pallas kernels: 36.3 us -> 35.8 us  [shards(): pl.pallas_call(functools.partial(kernel, (parts, shots, dom, sub, depth,...]
where the time goes in v3:
time: 37.9 us; the launch traced here: 37.7 us
  Pallas kernels  36.4 us (96%)
  between operations  1.29 us (3%)
    pallas_call x1, Pallas kernels, shards(): pl.pallas_call(functools.partial(kernel, (parts, shots, dom, sub, depth,...  35.8 us

profile of v3, /device:TPU:1, one launch (start us, length us, event | category | flops | bytes accessed | tf_op | source)
XLA Modules:
  0.0 37.7 jit_solution(6490207478270487064)
XLA Ops:
  1.3 35.8 %shard_map.131.both_ref = f32[40,8,128]{2,1,0:T(8,128)S(1)} custom-call(f32[8,8,128]{2,1,0:T(8,128)} %vel_in.1, bf16[1,32,8,128]{3,2,1,0:T(8,128)(2,1)} %prev_in.1, bf16[1,32,8,128]{3,2,1,0:T(8,128)(2,1)} %now_in.1, bf16[1,32,8,128]{3,2,1,0:T(8,128)(2,1)} %adjn_in.1, bf16[1,32,8,128]{3,2,1,0:T(8,128)(2,1)} %adj_in.1, s32[32,8,128]{2,1,0:T(8,128)} %sponge_in.1, ...), custom_call_target="tpu_custom_call" | custom-call | tf_op jit(solution)/shard_map/pallas_call | solution.py:466
  37.1 0.7 %shard_map.132 = (f32[8,8,128]{2,1,0:T(8,128)}, f32[1,32,8,128]{3,2,1,0:T(8,128)}) custom-call(f32[40,8,128]{2,1,0:T(8,128)S(1)} %shard_map.131.both_ref), custom_call_target="tpu_custom_call" | custom-call | tf_op jit(solution)/shard_map/pallas_call | solution.py:495

commit v4 on v3

--- a/solution.py
+++ b/solution.py
@@ -56,7 +56,9 @@
     return high, low
 
 
-N_SEMS = 22
+CHUNKS = 2
+AHEAD = 2
+N_SEMS = 20 + 2 * CHUNKS
 
 
 def kernel(
@@ -113,18 +115,21 @@
 
     far_cols, far_rows = pl.ds(0, (sub - 1) * cols), pl.ds(0, (dom - 1) * rows)
 
-    def field_send(ref, n):
-        state = group(ref.at[n, :, far_rows, 0:cols]), group(ref.at[n, :, :, far_cols])
-        here = ref.at[n, :, xs(d), ys(c)]
+    def field_send(ref, n, lo=0, size=None):
+        size = depth if size is None else size
+        part_of = pl.ds(lo, size)
+        state = group(ref.at[n, part_of, far_rows, 0:cols]), group(ref.at[n, part_of, :, far_cols])
+        here = ref.at[n, part_of, xs(d), ys(c)]
         for i in range(1, dom):
             put(state[0], here, here, {"dom": i})
         put_sub(state[1], here, here)
         return state
 
-    def field_relay(ref, n, state):
+    def field_relay(ref, n, state, lo=0, size=None):
+        part_of = pl.ds(lo, depth if size is None else size)
         take(state[0])
         for i in range(1, dom):
-            here = ref.at[n, :, xs(source("dom", i)), ys(c)]
+            here = ref.at[n, part_of, xs(source("dom", i)), ys(c)]
             put_sub(state[1], here, here)
 
     def in_slab(ref):
@@ -134,8 +139,8 @@
         lo = b * zb
         acc = None
         for part_of in (0,) if exact else (0, 1):
-            near = H[slot, part_of, lo : lo + zb + 2 * reach, :, lanes].reshape((zb + 2 * reach) * X, -1)
-            mid = H[slot, part_of, lo + reach : lo + reach + zb].reshape(zb * X, Y)
+            near = H[slot, part_of, pl.ds(lo, zb + 2 * reach), :, lanes].reshape((zb + 2 * reach) * X, -1)
+            mid = H[slot, part_of, pl.ds(lo + reach, zb)].reshape(zb * X, Y)
             term = jnp.dot(zx_ref[...], near, preferred_element_type=F32)
             acc = term if acc is None else acc + term
             acc = acc + jnp.dot(mid, ym_ref[:, lanes], preferred_element_type=F32)
@@ -202,7 +207,9 @@
     adj_state = field_send(L, 1)
     loads[3].wait()
     L[0, :, own_x, own_y] = adjn_ref[0].astype(F32)
-    adjn_state = field_send(L, 0)
+    chunks = CHUNKS if blocks % CHUNKS == 0 else 1
+    long = depth // chunks
+    adjn_state = [field_send(L, 0, i * long, long) for i in range(chunks)]
     for z in range(depth):
         PC[z] = jnp.zeros((X, Y), F32)
     for load in loads[4:]:
@@ -281,20 +288,20 @@
 
     whole_x, whole_y = slice(None), slice(None)
 
-    def advance(ref, n, slot, plane, at, ready=False):
+    def step(ref, n, slot, plane, at, b, ready):
+        acc = None if ready else neighbours(slot, b, False)
+        for i in range(zb):
+            z = b * zb + i
+            lap = (ACC[z] if ready else acc[i]) + centre * ref[n, z]
+            value = carried(ref, n, z, whole_x, whole_y) + KP[z] * lap
+            if z == at:
+                value = value + IV[z] * plane()
+            ref[n + 1, z] = value
+            keep(slot ^ 1, z, value)
+
+    for n in range(NF):
         for b in range(blocks):
-            acc = None if ready else neighbours(slot, b, False)
-            for i in range(zb):
-                z = b * zb + i
-                lap = (ACC[z] if ready else acc[i]) + centre * ref[n, z]
-                value = carried(ref, n, z, whole_x, whole_y) + KP[z] * lap
-                if z == at:
-                    value = value + IV[z] * plane
-                ref[n + 1, z] = value
-                keep(slot ^ 1, z, value)
-
-    for n in range(NF):
-        advance(U, n + 1, n % 2, src_hot * (0.5 * amp_at(n)), src_depth, n == 0)
+            step(U, n + 1, n % 2, lambda: src_hot * (0.5 * amp_at(n)), src_depth, b, n == 0)
         if n == max(0, NF - 2):
             field_relay(L, 1, adj_state)
 
@@ -309,7 +316,6 @@
         keep(2, z, L[1, z], True)
     for b in range(blocks):
         ACC[b * zb : (b + 1) * zb] = neighbours(2, b, True)
-    field_relay(L, 0, adjn_state)
     far_first = sorted(range(1, shots), key=lambda j: -min(j, shots - j))
 
     def to_owners(f):
@@ -319,31 +325,48 @@
         return idx
 
     illum_parts = to_owners(1)
-    take(adjn_state[1])
-
     def plane_of(n):
         return 0.5 * (CNT[...] * U[n + 1, rec_depth] - OB[n - 1])
 
-    for n in range(NF, 1, -1):
-        advance(L, NF + 1 - n, 2 + (NF - n) % 2, plane_of(n), rec_depth, n == NF)
-
     last = NF
-    for b in range(blocks):
-        ACC[b * zb : (b + 1) * zb, :, 0:cols] = neighbours(2 + (NF - 1) % 2, b, False, own_y)
+
+    def image(b):
+        lo = b * zb
+        ACC[pl.ds(lo, zb), :, 0:cols] = neighbours(2 + (NF - 1) % 2, b, False, own_y)
+        for i in range(zb):
+            z = lo + i
+            lap = ACC[z, own_x, 0:cols] + centre * L[last, z, own_x, own_y]
+            lam = carried(L, last, z, own_x, own_y) + KP[z, own_x, own_y] * lap
+            if i == rec_depth % zb:
+                here = jnp.where(z == rec_depth, 1.0, 0.0)
+                lam = lam + here * (IV[z, own_x, own_y] * SR[0, own_x, own_y])
+            u = [U[n, z, own_x, own_y] for n in range(NF + 2)]
+            grad = lam * (u[2] - 2.0 * u[1] + u[0])
+            for n in range(1, NF):
+                grad = grad + L[NF + 1 - n, z, own_x, own_y] * (u[n + 2] - 2.0 * u[n + 1] + u[n])
+            GI[0, z] = grad
+
+    for chunk in range(chunks):
+        for following in range(chunk, min(chunk + AHEAD, chunks)):
+            if following >= chunk + AHEAD - 1 or chunk == 0:
+                field_relay(L, 0, adjn_state[following], following * long, long)
+        take(adjn_state[chunk][1])
+        for b in range(chunk * blocks // chunks, (chunk + 1) * blocks // chunks):
+            step(L, 1, 2, lambda: plane_of(NF), rec_depth, b, True)
+    for q in range(1, NF - 1):
+        for b in range(blocks):
+            step(L, 1 + q, 2 + q % 2, lambda: plane_of(NF - q), rec_depth, b, False)
     SR[0] = plane_of(1)
-    source_plane = SR[0, own_x, own_y]
-    for z in range(depth):
-        lap = ACC[z, own_x, 0:cols] + centre * L[last, z, own_x, own_y]
-        lam = carried(L, last, z, own_x, own_y) + KP[z, own_x, own_y] * lap
-        if z == rec_depth:
-            lam = lam + IV[z, own_x, own_y] * source_plane
-        u = [U[n, z, own_x, own_y] for n in range(NF + 2)]
-        grad = lam * (u[2] - 2.0 * u[1] + u[0])
-        for n in range(1, NF):
-            grad = grad + L[NF + 1 - n, z, own_x, own_y] * (u[n + 2] - 2.0 * u[n + 1] + u[n])
-        GI[0, z] = grad
-
-    grad_parts = to_owners(0)
+    if owned == zb:
+        grad_parts = group(GR.at[0])
+        for j in far_first + [0]:
+            image(peer("shots", j))
+            if j:
+                put(grad_parts, GI.at[0, pl.ds(peer("shots", j) * owned, owned)], GR.at[0, j - 1], {"shots": j})
+    else:
+        for b in range(blocks):
+            image(b)
+        grad_parts = to_owners(0)
     plane = src_hot * (0.5 * amp_at(NF))
     for b in range(blocks):
         acc = neighbours(NF % 2, b, False)
@@ -437,10 +460,14 @@
         whole_group(idx).wait_send()
 
 
-def part(both_ref, dir_ref, out_ref):
-    owned = dir_ref.shape[0]
-    dir_ref[...] = both_ref[0:owned]
-    out_ref[0] = both_ref[owned:]
+def part(both_ref, dir_ref, out_ref, sems):
+    owned, depth = dir_ref.shape[0], out_ref.shape[1]
+    first = pltpu.make_async_copy(both_ref.at[pl.ds(0, owned)], dir_ref, sems.at[0])
+    second = pltpu.make_async_copy(both_ref.at[pl.ds(owned, depth)], out_ref.at[0], sems.at[1])
+    second.start()
+    first.start()
+    second.wait()
+    first.wait()
 
 
 def solution(mesh):
@@ -499,7 +526,8 @@
                 jax.ShapeDtypeStruct((1, depth, rows, cols), F32),
             ),
             in_specs=[vm],
-            out_specs=(vm, vm),
+            out_specs=(pl.BlockSpec(memory_space=pl.ANY), pl.BlockSpec(memory_space=pl.ANY)),
+            scratch_shapes=[pltpu.SemaphoreType.DMA((2,))],
             compiler_params=pltpu.CompilerParams(vmem_limit_bytes=VM_PART),
         )(both))
 

time: 37.9 us -> 37.5 us (0.989)
  no operation moved by 1% of the time
where the time goes in v4:
time: 37.5 us; the launch traced here: 37.4 us
  Pallas kernels  36.1 us (96%)
  between operations  1.29 us (3%)
    pallas_call x1, Pallas kernels, shards(): pl.pallas_call(functools.partial(kernel, (parts, shots, dom, sub, depth,...  35.4 us

profile of v4, /device:TPU:1, one launch (start us, length us, event | category | flops | bytes accessed | tf_op | source)
XLA Modules:
  0.0 37.4 jit_solution(10387931547930024021)
XLA Ops:
  1.3 35.4 %shard_map.131.both_ref = f32[40,8,128]{2,1,0:T(8,128)S(1)} custom-call(f32[8,8,128]{2,1,0:T(8,128)} %vel_in.1, bf16[1,32,8,128]{3,2,1,0:T(8,128)(2,1)} %prev_in.1, bf16[1,32,8,128]{3,2,1,0:T(8,128)(2,1)} %now_in.1, bf16[1,32,8,128]{3,2,1,0:T(8,128)(2,1)} %adjn_in.1, bf16[1,32,8,128]{3,2,1,0:T(8,128)(2,1)} %adj_in.1, s32[32,8,128]{2,1,0:T(8,128)} %sponge_in.1, ...), custom_call_target="tpu_custom_call" | custom-call | tf_op jit(solution)/shard_map/pallas_call | solution.py:493
  36.7 0.7 %shard_map.132 = (f32[8,8,128]{2,1,0:T(8,128)}, f32[1,32,8,128]{3,2,1,0:T(8,128)}) custom-call(f32[40,8,128]{2,1,0:T(8,128)S(1)} %shard_map.131.both_ref), custom_call_target="tpu_custom_call" | custom-call | tf_op jit(solution)/shard_map/pallas_call | solution.py:522

commit v5 on v4

--- a/solution.py
+++ b/solution.py
@@ -58,7 +58,7 @@
 
 CHUNKS = 2
 AHEAD = 2
-N_SEMS = 20 + 2 * CHUNKS
+N_SEMS = 19 + 2 * CHUNKS
 
 
 def kernel(
@@ -66,7 +66,7 @@
     vel_in, prev_in, now_in, adjn_in, adj_in, sponge_in, amp_in, src_ref, rec_in, obs_in, ym_in, zx_in,
     both_ref,
     prev_ref, now_ref, adjn_ref, adj_ref, amp_ref, rec_ref, obs_ref, ym_ref, zx_ref,
-    U, L, H, V, SP, IV, KP, ACC, PC, HS, HR, CR, OB, CNT, SR, GI, GR, ss, rs, ls,
+    U, L, H, V, SP, IV, KP, ACC, PC, HS, HR, OB, CNT, SR, GI, GR, ss, rs, ls,
 ):
     parts, shots, dom, sub, depth, rows, cols, owned, zb, sharing = sizes
     X, Y = dom * rows, sub * cols
@@ -160,7 +160,8 @@
     greeted = 0
     shifts = [{"shots": j, "dom": i, "sub": k} for j in range(shots) for i in range(dom) for k in range(sub)][1:]
     sharers = [{"groups": i, "shots": j} for j in range(shots) for i in range(parts if sharing > shots else 1)][1:sharing]
-    for shift in [shift for shift in sharers if shift["groups"]] + shifts:
+    shifts = [shift for shift in shifts if shift["dom"] or not (shift["shots"] and shift["sub"])]
+    for shift in shifts + [shift for shift in sharers if shift["groups"]]:
         pl.semaphore_signal(
             barrier, inc=1, device_id={axis: peer(axis, j) for axis, j in shift.items() if j}, device_id_type=MESH
         )
@@ -401,14 +402,14 @@
             idx = group(PC.at[pl.ds(0, len(members) * owned), 0:rows, 0:cols])
             column[idx] = members
     which = {j: idx for idx, members in column.items() for j in members}
-    beside, corner, cross = group(HR), group(CR), group(PC.at[:, 0:rows, far_cols])
+    beside, cross = group(HR), group(PC.at[:, 0:rows, far_cols])
     for j in far_first + [0]:
         if j:
             put(which[j], own, own, {"shots": j})
         for i in range(1, dom):
-            put(beside, HS.at[i - 1], HR.at[i - 1, s], {"dom": i, "shots": j})
+            put(beside, HS.at[i - 1], HR.at[i - 1, s, 0 : owned + 1], {"dom": i, "shots": j})
             for k in range(1, sub):
-                put(corner, HS.at[i - 1, owned], CR.at[i - 1, k - 1, s], {"dom": i, "shots": j, "sub": k})
+                put(beside, HS.at[i - 1, owned], HR.at[i - 1, s, owned + k], {"dom": i, "shots": j, "sub": k})
     put_sub(cross, own, own)
     for idx, members in column.items():
         take(idx)
@@ -422,13 +423,12 @@
     for k in range(1, sub):
         for z in range(depth):
             top = jnp.maximum(top, jnp.abs(PC[z, own_x, ys(source("sub", k))]))
-    take(corner)
     take(beside)
     rest = None
     for i in range(1, dom):
         across = xs(source("dom", i))
         for j in range(shots):
-            values = [HR[i - 1, j, owned]] + [CR[i - 1, k - 1, j] for k in range(1, sub)]
+            values = [HR[i - 1, j, owned + k] for k in range(sub)]
             for value in values:
                 rest = value if rest is None else jnp.maximum(rest, value)
         for z in range(depth):
@@ -504,8 +504,7 @@
                 pltpu.VMEM((4, 2, depth + 2 * reach, X, Y), BF16),
                 whole, pltpu.VMEM((depth, X, Y), jnp.int32), whole, whole, whole, whole,
                 pltpu.VMEM((max(1, dom - 1), owned + 1, reach, cols), F32),
-                pltpu.VMEM((max(1, dom - 1), shots, owned + 1, reach, cols), F32),
-                pltpu.VMEM((max(1, dom - 1), max(1, sub - 1), shots, reach, cols), F32),
+                pltpu.VMEM((max(1, dom - 1), shots, owned + sub, reach, cols), F32),
                 pltpu.VMEM((NF, X, Y), F32),
                 pltpu.VMEM((X, Y), F32),
                 pltpu.VMEM((2, X, Y), F32),

time: 37.5 us -> 37.7 us (level)
  no operation moved by 1% of the time
where the time goes in v5:
time: 37.7 us; the launch traced here: 37.5 us
  Pallas kernels  36.2 us (96%)
  between operations  1.29 us (3%)
    pallas_call x1, Pallas kernels, shards(): pl.pallas_call(functools.partial(kernel, (parts, shots, dom, sub, depth,...  35.5 us

profile of v5, /device:TPU:1, one launch (start us, length us, event | category | flops | bytes accessed | tf_op | source)
XLA Modules:
  0.0 37.5 jit_solution(17314149454795361683)
XLA Ops:
  1.3 35.5 %shard_map.131.both_ref = f32[40,8,128]{2,1,0:T(8,128)S(1)} custom-call(f32[8,8,128]{2,1,0:T(8,128)} %vel_in.1, bf16[1,32,8,128]{3,2,1,0:T(8,128)(2,1)} %prev_in.1, bf16[1,32,8,128]{3,2,1,0:T(8,128)(2,1)} %now_in.1, bf16[1,32,8,128]{3,2,1,0:T(8,128)(2,1)} %adjn_in.1, bf16[1,32,8,128]{3,2,1,0:T(8,128)(2,1)} %adj_in.1, s32[32,8,128]{2,1,0:T(8,128)} %sponge_in.1, ...), custom_call_target="tpu_custom_call" | custom-call | tf_op jit(solution)/shard_map/pallas_call | solution.py:493
  36.8 0.7 %shard_map.132 = (f32[8,8,128]{2,1,0:T(8,128)}, f32[1,32,8,128]{3,2,1,0:T(8,128)}) custom-call(f32[40,8,128]{2,1,0:T(8,128)S(1)} %shard_map.131.both_ref), custom_call_target="tpu_custom_call" | custom-call | tf_op jit(solution)/shard_map/pallas_call | solution.py:521
